TPU v7x, 512 devices: a whole 4x4x16 slice. The times are simulated.
512 devices in a mesh: gz: 32 (over z_lo, y), row: 16 (over z_hi, x, core).
Axes of the slice: x: 4, y: 4, z: 16 (z_hi: 2, z_lo: 8; z = z_hi * 8 + z_lo), core: 2. Of those that a mesh axis runs over, the one named last changes fastest.
Arguments:
- density: float32 [256, 128, 256], P('gz', 'row'), may hold values from 0.3 to 3
- pressure: float32 [256, 128, 256], P('gz', 'row'), may hold values from 0.3 to 3
- velocity: float32 [3, 256, 128, 256], P(None, 'gz', 'row'), may hold values from -3 to 3
- boundary: int32 [6], replicated, may hold values from 0 to 1
Outputs:
- density_out: float32 [256, 128, 256], P('gz', 'row')
- pressure_out: float32 [256, 128, 256], P('gz', 'row')
- velocity_out: float32 [3, 256, 128, 256], P(None, 'gz', 'row')
Inputs may be any that keep to these rules, and one draw needn't show every extreme that they name: `boundary`: 1 marks a reflecting face, 0 an outflow face; entries 2k and 2k+1 are the lower and upper faces of x, y, z in turn.
All inputs are finite; a program needn't handle non-finite values.
Results may differ from a plain program's by a relative error of at most 0.0003.
Values sent between devices are 32-bit elements; how exact they have to be, the bound alone decides.
No kernel may reach another device: no remote copies, remote signals or barrier semaphores. Data moves between devices by JAX's collectives and lax.ppermute only.
A program may use at most 64 MiB of HBM per device.

v0:
```python
import jax
import jax.numpy as jnp
import numpy as np
from jax import lax
from jax.sharding import PartitionSpec as P

RIEMANN_ITERS = 4


gamma_gas = 1.4
courant_ratio = 0.05
dens_floor = 0.02
press_floor = 0.02
star_frac = 0.1


def padded_2(cells, sides, width):
    for axis, dim in sides:
        count = lax.axis_size(axis)
        ends = count - 1
        head = lax.slice_in_dim(cells, 0, width, axis=dim)
        tail = lax.slice_in_dim(cells, cells.shape[dim] - width, cells.shape[dim], axis=dim)
        cells = jnp.concatenate(
            [
                lax.ppermute(tail, axis, [(i, (i + 1) % count) for i in range(ends)]),
                cells,
                lax.ppermute(head, axis, [((i + 1) % count, i) for i in range(ends)]),
            ],
            axis=dim,
        )
    return cells


def mirror_sign(normal, ndim):
    table = np.ones(5, np.float32)
    table[normal] = -1.0
    return jnp.asarray(table.reshape((5,) + (1,) * (ndim - 1)))


def normal_mask(normal, ndim):
    table = np.zeros(3, np.float32)
    table[normal - 2] = 1.0
    return jnp.asarray(table.reshape((3,) + (1,) * (ndim - 1)))


def boundary_cells(interior, along, face_flag, at_lower, normal):
    reflect = jnp.flip(interior, axis=along) * mirror_sign(normal, interior.ndim)
    edge_index = 0 if at_lower else 2
    edge_cell = lax.slice_in_dim(interior, edge_index, edge_index + 1, axis=along)
    outflow = jnp.concatenate([edge_cell, edge_cell, edge_cell], axis=along)
    return jnp.where(face_flag == 1, reflect, outflow)


def add_ghosts(fields, along, low_flag, high_flag, normal):
    inner_len = fields.shape[along]
    lower_ghosts = boundary_cells(
        lax.slice_in_dim(fields, 0, 3, axis=along), along, low_flag, True, normal
    )
    upper_ghosts = boundary_cells(
        lax.slice_in_dim(fields, inner_len - 3, inner_len, axis=along),
        along,
        high_flag,
        False,
        normal,
    )
    return jnp.concatenate([lower_ghosts, fields, upper_ghosts], axis=along)


def fix_edges(padded, along, low_flag, high_flag, at_first, at_last, normal):
    padded_len = padded.shape[along]
    lower_ghosts = boundary_cells(
        lax.slice_in_dim(padded, 3, 6, axis=along), along, low_flag, True, normal
    )
    upper_ghosts = boundary_cells(
        lax.slice_in_dim(padded, padded_len - 6, padded_len - 3, axis=along),
        along,
        high_flag,
        False,
        normal,
    )
    lower_ghosts = jnp.where(at_first, lower_ghosts, lax.slice_in_dim(padded, 0, 3, axis=along))
    upper_ghosts = jnp.where(
        at_last, upper_ghosts, lax.slice_in_dim(padded, padded_len - 3, padded_len, axis=along)
    )
    middle = lax.slice_in_dim(padded, 3, padded_len - 3, axis=along)
    return jnp.concatenate([lower_ghosts, middle, upper_ghosts], axis=along)


def conserved(prims):
    dens = prims[0:1]
    speeds = prims[2:5]
    energy = prims[1:2] / (gamma_gas - 1.0) + 0.5 * dens * jnp.sum(
        speeds * speeds, axis=0, keepdims=True
    )
    return jnp.concatenate([dens, energy, dens * speeds], axis=0)


def primitive(conserv):
    dens = jnp.maximum(conserv[0:1], dens_floor)
    speeds = conserv[2:5] / dens
    press = (gamma_gas - 1.0) * (
        conserv[1:2] - 0.5 * dens * jnp.sum(speeds * speeds, axis=0, keepdims=True)
    )
    return jnp.concatenate([dens, jnp.maximum(press, press_floor), speeds], axis=0)


def shock_side(star_press, side_press, sound_imp):
    ratio_g = (gamma_gas + 1.0) / (2.0 * gamma_gas)
    wave_speed = sound_imp * jnp.sqrt(1.0 + ratio_g * (star_press / side_press - 1.0))
    jump_speed = (star_press - side_press) / wave_speed
    jump_slope = (
        sound_imp
        * sound_imp
        * (1.0 + ratio_g * (star_press - side_press) / (2.0 * side_press))
        / wave_speed**3
    )
    return (jump_speed, jump_slope)


def godunov(left_state, right_state, normal):
    dens_left, dens_right = (left_state[0], right_state[0])
    press_left, press_right = (left_state[1], right_state[1])
    normal_left, normal_right = (left_state[normal], right_state[normal])
    sound_left = jnp.sqrt(gamma_gas * press_left * dens_left)
    sound_right = jnp.sqrt(gamma_gas * press_right * dens_right)
    floor_press = star_frac * jnp.minimum(press_left, press_right)
    star_press = (
        sound_right * press_left
        + sound_left * press_right
        - sound_left * sound_right * (normal_right - normal_left)
    ) / (sound_left + sound_right)
    star_press = jnp.maximum(star_press, floor_press)
    for attempt in range(RIEMANN_ITERS):
        jump_left, slope_left = shock_side(star_press, press_left, sound_left)
        jump_right, slope_right = shock_side(star_press, press_right, sound_right)
        star_press = star_press - (normal_right - normal_left + jump_left + jump_right) / (
            slope_left + slope_right
        )
        star_press = jnp.maximum(star_press, floor_press)
    jump_left, slope_left = shock_side(star_press, press_left, sound_left)
    jump_right, slope_right = shock_side(star_press, press_right, sound_right)
    star_speed = 0.5 * (normal_left - jump_left + (normal_right + jump_right))
    upwind = star_speed > 0.0
    dens_up = jnp.where(upwind, dens_left, dens_right)
    press_up = jnp.where(upwind, press_left, press_right)
    selector = normal_mask(normal, left_state.ndim)
    vel_up = jnp.where(upwind[None], left_state[2:5], right_state[2:5])
    vel_up = selector * star_speed[None] + (1.0 - selector) * vel_up
    energy_up = press_up / (gamma_gas - 1.0) + 0.5 * dens_up * jnp.sum(vel_up * vel_up, axis=0)
    mass_flux = dens_up * star_speed
    energy_flux = (energy_up + star_press) * star_speed
    moment_flux = mass_flux[None] * vel_up + selector * star_press[None]
    return jnp.concatenate([mass_flux[None], energy_flux[None], moment_flux], axis=0)


def sweep_cells(padded, along, normal):
    inner_len = padded.shape[along] - 6

    def window(start, length):
        return lax.slice_in_dim(padded, start, start + length, axis=along)

    left_in = window(1, inner_len + 3)
    right_in = window(2, inner_len + 3)
    interfaces = (
        7.0 * (left_in + right_in) - (window(0, inner_len + 3) + window(3, inner_len + 3))
    ) / 12.0
    interfaces = jnp.clip(
        interfaces, jnp.minimum(left_in, right_in), jnp.maximum(left_in, right_in)
    )
    centres = window(2, inner_len + 2)
    to_left = lax.slice_in_dim(interfaces, 0, inner_len + 2, axis=along) - centres
    to_right = lax.slice_in_dim(interfaces, 1, inner_len + 3, axis=along) - centres
    west_edge = centres + jnp.clip(to_left, -2.0 * jnp.abs(to_right), 2.0 * jnp.abs(to_right))
    east_edge = centres + jnp.clip(to_right, -2.0 * jnp.abs(to_left), 2.0 * jnp.abs(to_left))
    left_state = lax.slice_in_dim(east_edge, 0, inner_len + 1, axis=along)
    right_state = lax.slice_in_dim(west_edge, 1, inner_len + 2, axis=along)
    fluxes = godunov(left_state, right_state, normal)
    conserv = conserved(window(3, inner_len))
    conserv = conserv - courant_ratio * (
        lax.slice_in_dim(fluxes, 1, inner_len + 1, axis=along)
        - lax.slice_in_dim(fluxes, 0, inner_len, axis=along)
    )
    return primitive(conserv)


def z_sweep(fields, boundary):
    padded = padded_2(fields, (("gz", 1),), 3)
    at_first = lax.axis_index("gz") == 0
    at_last = lax.axis_index("gz") == lax.axis_size("gz") - 1
    padded = fix_edges(padded, 1, boundary[4], boundary[5], at_first, at_last, 4)
    return sweep_cells(padded, 1, 4)


def return_rows(fields):
    return lax.all_to_all(fields, "row", split_axis=2, concat_axis=3, tiled=True)


def on_device(density, pressure, velocity, boundary):
    fields = jnp.concatenate([density[None], pressure[None], velocity], axis=0)
    fields = sweep_cells(add_ghosts(fields, 3, boundary[0], boundary[1], 2), 3, 2)
    turned = jnp.swapaxes(
        lax.all_to_all(fields, "row", split_axis=3, concat_axis=2, tiled=True), 2, 3
    )
    columns = sweep_cells(add_ghosts(turned, 3, boundary[2], boundary[3], 3), 3, 3)
    fields = z_sweep(return_rows(jnp.swapaxes(columns, 2, 3)), boundary)
    return (fields[0], fields[1], fields[2:5])


def solution(mesh):
    in_specs = (P("gz", "row", None), P("gz", "row", None), P(None, "gz", "row", None), P())
    out_specs = (P("gz", "row", None), P("gz", "row", None), P(None, "gz", "row", None))
    return jax.shard_map(
        on_device, mesh=mesh, in_specs=in_specs, out_specs=out_specs, check_vma=False
    )
```

profile of v0, /device:TPU:24, one launch (start us, length us, event | category | flops | bytes accessed | tf_op | source)
XLA Modules:
  0.0 135.5 jit_solution(8363824731809600280)
XLA Ops:
  0.7 1.1 fusion.16
  2.0 1.0 multiply_reduce_fusion.8
  6.9 1.2 fusion.132
  8.9 3.1 %copy.187 = f32[5,8,8,256]{2,1,0,3:T(8,128)} copy(f32[5,8,8,256]{3,2,1,0:T(8,128)S(1)} %pad_maximum_fusion.8) | data formatting | bytes 655360 | tf_op jit(solution)/shard_map/concatenate | solution.py:104
  12.0 5.3 %reshape.81 = f32[16,1,5120]{2,1,0:T(1,128)} reshape(f32[256,5,8,8]{3,2,1,0:T(8,128)} %bitcast.119) | data formatting | bytes 655360
  17.3 17.7 %all-to-all-start = ((f32[16,1,5120]{2,1,0:T(1,128)}), f32[16,1,5120]{2,1,0:T(1,128)S(1)}, u32[]{:S(2)}, u32[]{:S(2)}) async-start(f32[16,1,5120]{2,1,0:T(1,128)} %reshape.81), calls=%async_computation | async-start | bytes 655360 | tf_op jit(solution)/shard_map/all_to_all | solution.py:202
  36.2 16.7 %all-to-all-done = f32[16,1,5120]{2,1,0:T(1,128)S(1)} async-done(((f32[16,1,5120]{2,1,0:T(1,128)}), f32[16,1,5120]{2,1,0:T(1,128)S(1)}, u32[]{:S(2)}, u32[]{:S(2)}) %all-to-all-start) | async-done | bytes 327712 | tf_op jit(solution)/shard_map/all_to_all | solution.py:202
  53.4 1.4 %reduce.5 = f32[16,5120]{1,0:T(8,128)S(1)} reduce(f32[16,1,5120]{2,1,0:T(1,128)S(1)} %all-to-all-done, f32[]{:T(128)} %broadcast.1082), dimensions={1}, to_apply=%all_to_all.26.reduce_sub_computation | reduce | bytes 655364 | tf_op jit(solution)/shard_map/all_to_all | solution.py:202
  54.9 4.4 %reshape.82 = f32[256,5,8,8]{3,2,1,0:T(8,128)} reshape(f32[16,5120]{1,0:T(8,128)S(1)} %reduce.5) | data formatting | bytes 655360
  59.3 4.2 %copy.188 = f32[5,8,8,16,16]{4,2,3,1,0:T(8,128)S(1)} copy(f32[5,8,8,16,16]{2,1,0,4,3:T(8,128)} %bitcast.120) | data formatting | bytes 655360 | tf_op jit(solution)/shard_map/all_to_all | solution.py:202
  63.4 0.7 copy.189
  66.7 1.6 %fusion.131 = (pred[8,16,129]{2,1,0:T(8,128)(4,1)S(1)}, f32[1,8,16,129]{3,2,1,0:T(8,128)S(1)}, f32[1,8,16,129]{3,2,1,0:T(8,128)S(1)}) fusion(f32[5,8,16,130]{3,2,1,0:T(8,128)S(1)} %get-tuple-element.33, f32[5,8,16,130]{3,2,1,0:T(8,128)S(1)} %get-tuple-element.32), kind=kLoop, calls=%fused_computation.271 | loop fusion | flops 2889600 | bytes 544896 | tf_op jit(solution)/shard_map/jit(_where)/broadcast_in_dim | solution.py:147
  69.1 0.8 copy.190
  70.0 1.7 %reshape.83 = f32[16,1,5120]{2,1,0:T(1,128)} reshape(f32[128,5,8,16]{3,2,1,0:T(8,128)S(1)} %bitcast.123) | data formatting | bytes 655360
  71.6 3.8 %all-to-all-start.1 = ((f32[16,1,5120]{2,1,0:T(1,128)}), f32[16,1,5120]{2,1,0:T(1,128)S(1)}, u32[]{:S(2)}, u32[]{:S(2)}) async-start(f32[16,1,5120]{2,1,0:T(1,128)} %reshape.83), calls=%async_computation.1 | async-start | bytes 655360 | tf_op jit(solution)/shard_map/all_to_all | solution.py:195
  76.6 16.0 %all-to-all-done.1 = f32[16,1,5120]{2,1,0:T(1,128)S(1)} async-done(((f32[16,1,5120]{2,1,0:T(1,128)}), f32[16,1,5120]{2,1,0:T(1,128)S(1)}, u32[]{:S(2)}, u32[]{:S(2)}) %all-to-all-start.1) | async-done | bytes 327712 | tf_op jit(solution)/shard_map/all_to_all | solution.py:195
  92.6 1.4 %reduce.6 = f32[16,5120]{1,0:T(8,128)S(1)} reduce(f32[16,1,5120]{2,1,0:T(1,128)S(1)} %all-to-all-done.1, f32[]{:T(128)} %broadcast.1082), dimensions={1}, to_apply=%all_to_all.30.reduce_sub_computation | reduce | bytes 655364 | tf_op jit(solution)/shard_map/all_to_all | solution.py:195
  94.0 0.9 reshape.84
  95.4 2.2 %multiply_reduce_fusion = (f32[8,8,16,16]{3,1,2,0:T(8,128)}, f32[3,8,8,16,16]{4,2,3,1,0:T(8,128)}) fusion(f32[5,8,8,16,16]{4,2,3,1,0:T(8,128)S(1)} %bitcast.121), kind=kLoop, calls=%fused_computation.1 | loop fusion | flops 81920 | bytes 458752 | tf_op jit(solution)/shard_map/reduce_sum | solution.py:92
  97.6 0.9 slice_multiply_fusion
  98.6 0.9 mul.1862
  99.7 3.0 %copy.197 = f32[5,8,8,16,16]{4,3,2,1,0:T(8,128)} copy(f32[5,8,8,16,16]{4,1,0,2,3:T(8,128)S(1)} %bitcast.118) | data formatting | bytes 655360 | tf_op jit(solution)/shard_map/all_to_all | solution.py:195
  102.7 2.7 %all_to_all.33 = f32[5,8,8,256]{3,2,1,0:T(8,128)S(1)} reshape(f32[5,8,8,16,16]{4,3,2,1,0:T(8,128)} %copy.197) | data formatting | bytes 655360 | tf_op jit(solution)/shard_map/all_to_all | solution.py:195
  105.5 0.7 fusion.139
  106.2 15.8 %collective-permute-start = (f32[5,3,8,256]{3,2,1,0:T(8,128)}, f32[5,3,8,256]{3,2,1,0:T(8,128)}, u32[]{:S(2)}, u32[]{:S(2)}) collective-permute-start(f32[5,3,8,256]{3,2,1,0:T(8,128)} %get-tuple-element.44), channel_id=1, source_target_pairs={{0,16},{16,32},{32,48},{48,64},{64,80},{80,96},{96,112},{112,128},... | collective-permute-start | bytes 368648 | tf_op jit(solution)/shard_map/ppermute | solution.py:25
  122.0 1.9 %collective-permute-start.1 = (f32[5,3,8,256]{3,2,1,0:T(8,128)}, f32[5,3,8,256]{3,2,1,0:T(8,128)}, u32[]{:S(2)}, u32[]{:S(2)}) collective-permute-start(f32[5,3,8,256]{3,2,1,0:T(8,128)} %get-tuple-element.45), channel_id=1, source_target_pairs={{16,0},{32,16},{48,32},{64,48},{80,64},{96,80},{112,96},{128,112},... | collective-permute-start | bytes 368648 | tf_op jit(solution)/shard_map/ppermute | solution.py:27
  124.2 0.7 slice.362
  124.9 1.1 copy.193
  126.7 4.6 %collective-permute-done.1 = f32[5,3,8,256]{3,2,1,0:T(8,128)} collective-permute-done((f32[5,3,8,256]{3,2,1,0:T(8,128)}, f32[5,3,8,256]{3,2,1,0:T(8,128)}, u32[]{:S(2)}, u32[]{:S(2)}) %collective-permute-start.1) | collective-permute-done | bytes 122912 | tf_op jit(solution)/shard_map/ppermute | solution.py:27
  131.3 1.2 select_select_fusion.1
  132.9 0.8 fusion.133
  134.1 0.7 multiply_reduce_fusion.4
  (97 shorter events, 10.4 us)
Async XLA Ops:
  0.6 5.0 %copy-start.15 = (f32[5]{0:T(128)S(1)}, f32[5]{0:T(128)}, u32[]{:S(2)}) copy-start(f32[5]{0:T(128)} %constant.139) | copy-start | bytes 64
  0.6 5.2 %copy-start.2 = (f32[8,8,256]{2,1,0:T(8,128)S(1)}, f32[8,8,256]{2,1,0:T(8,128)}, u32[]{:S(2)}) copy-start(f32[8,8,256]{2,1,0:T(8,128)} %param.13) | copy-start | bytes 196612
  0.7 5.2 %copy-start.1 = (f32[3,8,8,256]{3,2,1,0:T(8,128)S(1)}, f32[3,8,8,256]{3,2,1,0:T(8,128)}, u32[]{:S(2)}) copy-start(f32[3,8,8,256]{3,2,1,0:T(8,128)} %param.15) | copy-start | bytes 589828
  0.7 5.2 %copy-start.4 = (f32[8,8,256]{2,1,0:T(8,128)S(1)}, f32[8,8,256]{2,1,0:T(8,128)}, u32[]{:S(2)}) copy-start(f32[8,8,256]{2,1,0:T(8,128)} %param.14) | copy-start | bytes 196612
  0.7 2.7 %copy-start.7 = (s32[6]{0:T(128)S(1)}, s32[6]{0:T(128)}, u32[]{:S(2)}) copy-start(s32[6]{0:T(128)} %param.16) | copy-start | bytes 76
  6.1 2.1 %copy-start.13 = (f32[3]{0:T(128)S(1)}, f32[3]{0:T(128)}, u32[]{:S(2)}) copy-start(f32[3]{0:T(128)} %constant.143) | copy-start | bytes 40
  6.1 2.1 %copy-start.14 = (f32[3]{0:T(128)S(1)}, f32[3]{0:T(128)}, u32[]{:S(2)}) copy-start(f32[3]{0:T(128)} %constant.140) | copy-start | bytes 40
  17.3 35.7 %all-to-all-start = ((f32[16,1,5120]{2,1,0:T(1,128)}), f32[16,1,5120]{2,1,0:T(1,128)S(1)}, u32[]{:S(2)}, u32[]{:S(2)}) async-start(f32[16,1,5120]{2,1,0:T(1,128)} %reshape.81), calls=%async_computation | async-start | bytes 655360 | tf_op jit(solution)/shard_map/all_to_all | solution.py:202
  63.4 1.6 %copy-start.12 = (f32[5]{0:T(128)S(1)}, f32[5]{0:T(128)}, u32[]{:S(2)}) copy-start(f32[5]{0:T(128)} %constant.144) | copy-start | bytes 64
  66.2 2.2 %copy-start.10 = (f32[3]{0:T(128)S(1)}, f32[3]{0:T(128)}, u32[]{:S(2)}) copy-start(f32[3]{0:T(128)} %constant.148) | copy-start | bytes 40
  66.2 2.2 %copy-start.11 = (f32[3]{0:T(128)S(1)}, f32[3]{0:T(128)}, u32[]{:S(2)}) copy-start(f32[3]{0:T(128)} %constant.145) | copy-start | bytes 40
  71.6 21.0 %all-to-all-start.1 = ((f32[16,1,5120]{2,1,0:T(1,128)}), f32[16,1,5120]{2,1,0:T(1,128)S(1)}, u32[]{:S(2)}, u32[]{:S(2)}) async-start(f32[16,1,5120]{2,1,0:T(1,128)} %reshape.83), calls=%async_computation.1 | async-start | bytes 655360 | tf_op jit(solution)/shard_map/all_to_all | solution.py:195
  102.7 21.2 %copy-start = (f32[3,8,8,16,16]{4,2,3,1,0:T(8,128)S(1)}, f32[3,8,8,16,16]{4,2,3,1,0:T(8,128)}, u32[]{:S(2)}) copy-start(f32[3,8,8,16,16]{4,2,3,1,0:T(8,128)} %get-tuple-element.27) | copy-start | bytes 589828
  106.2 20.5 %collective-permute-start = (f32[5,3,8,256]{3,2,1,0:T(8,128)}, f32[5,3,8,256]{3,2,1,0:T(8,128)}, u32[]{:S(2)}, u32[]{:S(2)}) collective-permute-start(f32[5,3,8,256]{3,2,1,0:T(8,128)} %get-tuple-element.44), channel_id=1, source_target_pairs={{0,16},{16,32},{32,48},{48,64},{64,80},{80,96},{96,112},{112,128},... | collective-permute-start | bytes 368648 | tf_op jit(solution)/shard_map/ppermute | solution.py:25
  122.0 9.3 %collective-permute-start.1 = (f32[5,3,8,256]{3,2,1,0:T(8,128)}, f32[5,3,8,256]{3,2,1,0:T(8,128)}, u32[]{:S(2)}, u32[]{:S(2)}) collective-permute-start(f32[5,3,8,256]{3,2,1,0:T(8,128)} %get-tuple-element.45), channel_id=1, source_target_pairs={{16,0},{32,16},{48,32},{64,48},{80,64},{96,80},{112,96},{128,112},... | collective-permute-start | bytes 368648 | tf_op jit(solution)/shard_map/ppermute | solution.py:27
  124.2 2.1 %copy-start.3 = (f32[8,8,16,16]{3,1,2,0:T(8,128)S(1)}, f32[8,8,16,16]{3,1,2,0:T(8,128)}, u32[]{:S(2)}) copy-start(f32[8,8,16,16]{3,1,2,0:T(8,128)} %get-tuple-element.26) | copy-start | bytes 196612
  124.2 2.4 %copy-start.5 = (f32[8,8,256]{2,1,0:T(8,128)S(1)}, f32[8,8,256]{2,1,0:T(8,128)}, u32[]{:S(2)}) copy-start(f32[8,8,256]{2,1,0:T(8,128)} %mul.1862) | copy-start | bytes 196612
  124.2 7.1 %copy-start.16 = (f32[5]{0:T(128)S(1)}, f32[5]{0:T(128)}, u32[]{:S(2)}) copy-start(f32[5]{0:T(128)} %constant.149) | copy-start | bytes 64
  132.6 1.3 copy-start.8
  132.6 1.3 copy-start.9
  134.1 1.4 %copy-start.6 = (f32[8,8,256]{2,1,0:T(8,128)}, f32[8,8,256]{2,1,0:T(8,128)S(1)}, u32[]{:S(2)}) copy-start(f32[8,8,256]{2,1,0:T(8,128)S(1)} %fusion.127) | copy-start | bytes 196612
where the time goes:
time: 136 us
  starting transfers between devices  39.1 us (29%)
  waiting for transfers between devices  37.3 us (27%)
  local copies, waits for them, and re-layouts  34.9 us (26%)
  other arithmetic  19.1 us (14%)
  between operations  5.07 us (4%)
    all_to_all x1, starting transfers between devices, on_device(): lax.all_to_all(fields, 'row', split_axis=3, concat_axis=2, tiled=True)  17.7 us
    all_to_all x1, waiting for transfers between devices, on_device(): lax.all_to_all(fields, 'row', split_axis=3, concat_axis=2, tiled=True)  16.7 us
    all_to_all x1, waiting for transfers between devices, return_rows(): lax.all_to_all(fields, 'row', split_axis=2, concat_axis=3, tiled=True)  16 us
    ppermute x1, starting transfers between devices, padded_2(): lax.ppermute(tail, axis, [(i, (i + 1) % count) for i in range(ends)])  15.8 us
    unnamed x40, local copies, waits for them, and re-layouts  12.9 us
    all_to_all x3, local copies, waits for them, and re-layouts, return_rows(): lax.all_to_all(fields, 'row', split_axis=2, concat_axis=3, tiled=True)  6.24 us
    all_to_all x3, local copies, waits for them, and re-layouts, on_device(): lax.all_to_all(fields, 'row', split_axis=3, concat_axis=2, tiled=True)  5.37 us
    ppermute x1, waiting for transfers between devices, padded_2(): lax.ppermute(head, axis, [((i + 1) % count, i) for i in range(ends)])  4.58 us
  transfers between devices with their start and end apart: 4, of which 3 were waited for; matrix products, arithmetic and copies ran while one was open for 2% of the time, Pallas kernels for 0%

commit v1 on v0

v1 whole, which is shorter than its diff:
```python
import functools

import jax
import jax.numpy as jnp
from jax import lax
from jax.experimental import pallas as pl
from jax.experimental.pallas import tpu as pltpu
from jax.sharding import PartitionSpec as P

RIEMANN_ITERS = 4
GAMMA = 1.4
COURANT = 0.05
DENS_FLOOR = 0.02
PRESS_FLOOR = 0.02
STAR_FRAC = 0.1
RATIO_G = (GAMMA + 1.0) / (2.0 * GAMMA)
WIDTH = 3
LANES = 128


def face_value(far_left, left, right, far_right):
    value = (7.0 / 12.0) * (left + right) - (1.0 / 12.0) * (far_left + far_right)
    return jnp.clip(value, jnp.minimum(left, right), jnp.maximum(left, right))


def cell_edges(cell, face_left, face_right):
    to_left = face_left - cell
    to_right = face_right - cell
    two_left = 2.0 * jnp.abs(to_left)
    two_right = 2.0 * jnp.abs(to_right)
    west = cell + jnp.clip(to_left, -two_right, two_right)
    east = cell + jnp.clip(to_right, -two_left, two_left)
    return west, east


def godunov(left, right):
    rho_l, p_l, u_l, s_l, t_l = left
    rho_r, p_r, u_r, s_r, t_r = right
    inv_l = lax.rsqrt(GAMMA * (p_l * rho_l))
    inv_r = lax.rsqrt(GAMMA * (p_r * rho_r))
    jump = u_r - u_l
    floor = STAR_FRAC * jnp.minimum(p_l, p_r)
    star = (inv_l * p_l + inv_r * p_r - jump) / (inv_l + inv_r)
    star = jnp.maximum(star, floor)
    slope_l = RATIO_G / p_l
    slope_r = RATIO_G / p_r

    def side(star, p, inv, slope):
        root = lax.rsqrt((1.0 - RATIO_G) + slope * star)
        scaled = inv * root
        return root, scaled, (star - p) * scaled

    for _ in range(RIEMANN_ITERS):
        root_l, scaled_l, f_l = side(star, p_l, inv_l, slope_l)
        root_r, scaled_r, f_r = side(star, p_r, inv_r, slope_r)
        twice = scaled_l * (1.0 + root_l * root_l) + scaled_r * (1.0 + root_r * root_r)
        star = star - 2.0 * (jump + f_l + f_r) / twice
        star = jnp.maximum(star, floor)
    _, _, f_l = side(star, p_l, inv_l, slope_l)
    _, _, f_r = side(star, p_r, inv_r, slope_r)
    speed = 0.5 * ((u_l - f_l) + (u_r + f_r))
    upwind = speed > 0.0
    rho = jnp.where(upwind, rho_l, rho_r)
    p = jnp.where(upwind, p_l, p_r)
    s = jnp.where(upwind, s_l, s_r)
    t = jnp.where(upwind, t_l, t_r)
    mass = rho * speed
    energy = p * (1.0 / (GAMMA - 1.0)) + 0.5 * rho * (speed * speed + s * s + t * t)
    return (mass, (energy + star) * speed, mass * speed + star, mass * s, mass * t)


def advance(cell, flux_low, flux_high):
    rho, p, u, s, t = cell
    change = [COURANT * (high - low) for low, high in zip(flux_low, flux_high)]
    mass = rho - change[0]
    energy = p * (1.0 / (GAMMA - 1.0)) + 0.5 * rho * (u * u + s * s + t * t) - change[1]
    mom = [rho * v - c for v, c in zip((u, s, t), change[2:])]
    rho = jnp.maximum(mass, DENS_FLOOR)
    inv = 1.0 / rho
    u, s, t = (m * inv for m in mom)
    p = (GAMMA - 1.0) * (energy - 0.5 * rho * (u * u + s * s + t * t))
    return rho, jnp.maximum(p, PRESS_FLOOR), u, s, t


def field_order(normal):
    return (0, 1, normal) + tuple(v for v in (2, 3, 4) if v != normal)


def sign_of(flag):
    return jnp.where(flag == 1, -1.0, 1.0).astype(jnp.float32)


def x_kernel(
    flags, index, dens, press, vel, main, first, second, left, right, turn
):
    planes, rows, cells = dens.shape
    pair = 2
    half = cells // LANES
    lane = lax.broadcasted_iota(jnp.int32, (pair * rows, cells), 1)
    short = lax.broadcasted_iota(jnp.int32, (rows, LANES), 1)
    sign_low, sign_high = sign_of(flags[0]), sign_of(flags[1])

    def load(field, start):
        ref = (dens, press, vel.at[0], vel.at[1], vel.at[2])[field]
        return ref[start : start + pair].reshape(pair * rows, cells)

    edge = [jnp.zeros((rows, LANES), jnp.float32) for _ in range(5)]
    for start in range(0, planes, pair):
        block = slice(start * rows, (start + pair) * rows)
        for field in range(5):
            low = sign_low if field == 2 else 1.0
            high = sign_high if field == 2 else 1.0
            cell = load(field, start)
            before = jnp.where(lane == 0, low * cell, pltpu.roll(cell, 1, 1))
            after = jnp.where(lane == cells - 1, high * cell, pltpu.roll(cell, cells - 1, 1))
            face = face_value(pltpu.roll(before, 1, 1), before, cell, after)
            face = jnp.where(lane == 0, 0.5 * (before + cell), face)
            face_next = jnp.where(
                lane == cells - 1, 0.5 * (cell + after), pltpu.roll(face, cells - 1, 1)
            )
            west, east = cell_edges(cell, face, face_next)
            left[field, block, :] = jnp.where(lane == 0, low * west, pltpu.roll(east, 1, 1))
            right[field, block, :] = west
            for k in range(pair):
                z = start + k
                last = east[k * rows : (k + 1) * rows, cells - LANES :]
                edge[field] = jnp.where(short == z, pltpu.roll(last, z + 1, 1), edge[field])
    wall = [jnp.where(short < planes, e, 1.0) for e in edge]
    wall_flux = godunov(wall, [w * sign_high if f == 2 else w for f, w in enumerate(wall)])

    for start in range(0, planes, pair):
        block = slice(start * rows, (start + pair) * rows)
        flux = godunov(
            [left[f, block, :] for f in range(5)], [right[f, block, :] for f in range(5)]
        )
        after = []
        for f in range(5):
            rolled = pltpu.roll(flux[f], cells - 1, 1)
            end = jnp.concatenate(
                [pltpu.roll(wall_flux[f], LANES - 1 - start - k, 1) for k in range(pair)], axis=0
            )
            tail = jnp.where(short_pair(short, pair) == LANES - 1, end, rolled[:, cells - LANES :])
            after.append(jnp.concatenate([rolled[:, : cells - LANES], tail], axis=1))
        new = advance([load(f, start) for f in range(5)], flux, after)
        for f in range(5):
            for h in range(half):
                base = ((f * half + h) * planes + start) * rows
                turn[base : base + pair * rows, :] = new[f][:, h * LANES : (h + 1) * LANES]
    turn_over(turn, main, half)
    edge_blocks(index[0], main, first, second)


def short_pair(short, pair):
    return jnp.concatenate([short] * pair, axis=0)


def turn_over(turn, main, half):
    fields, outer, inner, _ = main.shape
    for f in range(fields):
        for h in range(half):
            base = (f * half + h) * outer * inner
            for j in range(outer):
                main[f, j, :, h * LANES : (h + 1) * LANES] = turn[pl.ds(base + j, inner, stride=outer), :]


def edge_blocks(place, main, first, second):
    outer = main.shape[1]
    odd = lax.rem(place, 2) == 1
    start_first = jnp.where(odd, outer - WIDTH, 0)
    start_second = jnp.where(odd, 0, outer - WIDTH)
    for f in range(5):
        for k in range(WIDTH):
            first[f, k] = main[f, start_first + k]
            second[f, k] = main[f, start_second + k]


def sweep_outer(place, count, flag_low, flag_high, normal, main, first, second, ghost, left, right, flux, store):
    outer, rows, cells = main.shape[1:]
    half = cells // LANES
    odd = lax.rem(place, 2) == 1

    @pl.when(odd)
    def _():
        ghost[:, :WIDTH] = second[...]
        ghost[:, WIDTH:] = first[...]

    @pl.when(jnp.logical_not(odd))
    def _():
        ghost[:, :WIDTH] = first[...]
        ghost[:, WIDTH:] = second[...]

    def wall(slot, edge, step, flag):
        for f in range(5):
            sign = sign_of(flag) if f == normal else 1.0
            for k in range(WIDTH):
                ghost[f, slot(k)] = jnp.where(flag == 1, sign * main[f, edge + step * k], main[f, edge])

    @pl.when(place == 0)
    def _():
        wall(lambda k: WIDTH - 1 - k, 0, 1, flag_low)

    @pl.when(place == count - 1)
    def _():
        wall(lambda k: WIDTH + k, outer - 1, -1, flag_high)

    order = field_order(normal)
    for f in range(5):
        for h in range(half):
            part = slice(h * LANES, (h + 1) * LANES)

            def cell(i):
                if i < 0:
                    return ghost[f, WIDTH + i, :, part]
                if i >= outer:
                    return ghost[f, WIDTH + i - outer, :, part]
                return main[f, i, :, part]

            value = {i: cell(i) for i in range(-WIDTH, outer + WIDTH)}
            face = None
            for i in range(-1, outer + 1):
                if face is None:
                    face = face_value(*(value[i + d] for d in (-2, -1, 0, 1)))
                face_next = face_value(*(value[i + d] for d in (-1, 0, 1, 2)))
                west, east = cell_edges(value[i], face, face_next)
                if i < outer:
                    left[f, i + 1, :, part] = east
                if i >= 0:
                    right[f, i, :, part] = west
                face = face_next
    chunk = 3
    for start in range(0, outer + 1, chunk):
        stop = min(start + chunk, outer + 1)
        for h in range(half):
            part = slice(h * LANES, (h + 1) * LANES)
            out = godunov(
                [left[f, start:stop, :, part] for f in order],
                [right[f, start:stop, :, part] for f in order],
            )
            for f in range(5):
                flux[f, start:stop, :, part] = out[f]
    for i in range(outer):
        new = advance(
            [main[f, i] for f in order], [flux[f, i] for f in range(5)], [flux[f, i + 1] for f in range(5)]
        )
        store(i, {f: new[k] for k, f in enumerate(order)})


def y_kernel(flags, index, main, first, second, out, out_first, out_second, ghost, left, right, flux, turn, *, count):
    outer, rows, cells = main.shape[1:]
    half = cells // LANES

    def store(i, new):
        for f in range(5):
            for h in range(half):
                base = ((f * half + h) * outer + i) * rows
                turn[base : base + rows, :] = new[f][:, h * LANES : (h + 1) * LANES]

    sweep_outer(index[0], count, flags[2], flags[3], 3, main, first, second, ghost, left, right, flux, store)
    turn_over(turn, out, half)
    edge_blocks(index[1], out, out_first, out_second)


def z_kernel(flags, index, main, first, second, dens, press, vel, ghost, left, right, flux, *, count):
    def store(i, new):
        dens[i] = new[0]
        press[i] = new[1]
        for v in range(3):
            vel[v, i] = new[2 + v]

    sweep_outer(index[1], count, flags[4], flags[5], 4, main, first, second, ghost, left, right, flux, store)


def exchange(block, axis, start):
    pairs = []
    for i in range(start, lax.axis_size(axis) - 1, 2):
        pairs += [(i, i + 1), (i + 1, i)]
    return lax.ppermute(block, axis, pairs)


def on_device(density, pressure, velocity, boundary):
    planes, rows, cells = density.shape
    half = cells // LANES
    f32 = jnp.float32
    place = jnp.stack([lax.axis_index("row"), lax.axis_index("gz")]).astype(jnp.int32)
    smem = pl.BlockSpec(memory_space=pltpu.SMEM)
    vmem = pl.BlockSpec(memory_space=pltpu.VMEM)
    params = pltpu.CompilerParams(vmem_limit_bytes=32 << 20)
    by_y = jax.ShapeDtypeStruct((5, rows, planes, cells), f32)
    by_z = jax.ShapeDtypeStruct((5, planes, rows, cells), f32)
    y_edge = jax.ShapeDtypeStruct((5, WIDTH, planes, cells), f32)
    z_edge = jax.ShapeDtypeStruct((5, WIDTH, rows, cells), f32)
    turn = pltpu.VMEM((5 * half * planes * rows, LANES), f32)

    def work(outer, inner):
        return [
            pltpu.VMEM((5, 2 * WIDTH, inner, cells), f32),
            pltpu.VMEM((5, outer + 1, inner, cells), f32),
            pltpu.VMEM((5, outer + 1, inner, cells), f32),
            pltpu.VMEM((5, outer + 1, inner, cells), f32),
        ]

    main, first, second = pl.pallas_call(
        x_kernel,
        out_shape=(by_y, y_edge, y_edge),
        in_specs=[smem, smem, vmem, vmem, vmem],
        out_specs=(vmem, vmem, vmem),
        scratch_shapes=[
            pltpu.VMEM((5, planes * rows, cells), f32),
            pltpu.VMEM((5, planes * rows, cells), f32),
            turn,
        ],
        compiler_params=params,
        name="x_sweep",
    )(boundary, place, density, pressure, velocity)
    first = exchange(first, "row", 1)
    second = exchange(second, "row", 0)
    main, first, second = pl.pallas_call(
        functools.partial(y_kernel, count=lax.axis_size("row")),
        out_shape=(by_z, z_edge, z_edge),
        in_specs=[smem, smem, vmem, vmem, vmem],
        out_specs=(vmem, vmem, vmem),
        scratch_shapes=work(rows, planes) + [turn],
        compiler_params=params,
        name="y_sweep",
    )(boundary, place, main, first, second)
    first = exchange(first, "gz", 1)
    second = exchange(second, "gz", 0)
    return pl.pallas_call(
        functools.partial(z_kernel, count=lax.axis_size("gz")),
        out_shape=(
            jax.ShapeDtypeStruct(density.shape, f32),
            jax.ShapeDtypeStruct(pressure.shape, f32),
            jax.ShapeDtypeStruct(velocity.shape, f32),
        ),
        in_specs=[smem, smem, vmem, vmem, vmem],
        out_specs=(vmem, vmem, vmem),
        scratch_shapes=work(planes, rows),
        compiler_params=params,
        name="z_sweep",
    )(boundary, place, main, first, second)


def solution(mesh):
    in_specs = (P("gz", "row", None), P("gz", "row", None), P(None, "gz", "row", None), P())
    out_specs = (P("gz", "row", None), P("gz", "row", None), P(None, "gz", "row", None))
    return jax.shard_map(
        on_device, mesh=mesh, in_specs=in_specs, out_specs=out_specs, check_vma=False
    )
```

time: 136 us -> 43.9 us (0.32)
  the two profiles are of different devices: /device:TPU:24 before, /device:TPU:320 now
where the time goes in v1:
time: 43.9 us; the launch traced here: 43.6 us
  waiting for transfers between devices  17.7 us (40%)
  starting transfers between devices  15.3 us (35%)
  Pallas kernels  6.6 us (15%)
  local copies, waits for them, and re-layouts  3.18 us (7%)
  between operations  0.69 us (2%)
    ppermute x4, waiting for transfers between devices, exchange(): return lax.ppermute(block, axis, pairs)  17.7 us
    ppermute x4, starting transfers between devices, exchange(): return lax.ppermute(block, axis, pairs)  15.3 us
    unnamed x8, local copies, waits for them, and re-layouts  3.18 us
    pallas_call x1, Pallas kernels, on_device(): pl.pallas_call(x_kernel, out_shape=(by_y, y_edge, y_edge), in_specs=[smem...  2.95 us
    pallas_call x1, Pallas kernels, on_device(): pl.pallas_call(functools.partial(z_kernel, count=lax.axis_size('gz')), ou...  2.16 us
    pallas_call x1, Pallas kernels, on_device(): pl.pallas_call(functools.partial(y_kernel, count=lax.axis_size('row')), o...  1.48 us
  transfers between devices with their start and end apart: 4, of which 3 were waited for; matrix products, arithmetic and copies ran while one was open for 0% of the time, Pallas kernels for 0%

profile of v1, /device:TPU:320, one launch (start us, length us, event | category | flops | bytes accessed | tf_op | source)
XLA Modules:
  0.0 43.6 jit_solution(11617514516433615684)
XLA Ops:
  0.6 0.0 copy-start.3
  0.6 0.1 pad_add_fusion.index
  0.7 0.6 %copy-done.3 = s32[6]{0:T(128)S(1)} copy-done((s32[6]{0:T(128)S(1)}, s32[6]{0:T(128)}, u32[]{:S(2)}) %copy-start.3) | copy-done | bytes 48
  1.3 0.0 copy-start
  1.3 0.9 %copy-done = f32[3,8,8,256]{3,2,1,0:T(8,128)S(1)} copy-done((f32[3,8,8,256]{3,2,1,0:T(8,128)S(1)}, f32[3,8,8,256]{3,2,1,0:T(8,128)}, u32[]{:S(2)}) %copy-start) | copy-done | bytes 196632
  2.2 0.0 copy-start.1
  2.2 0.8 %copy-done.1 = f32[8,8,256]{2,1,0:T(8,128)S(1)} copy-done((f32[8,8,256]{2,1,0:T(8,128)S(1)}, f32[8,8,256]{2,1,0:T(8,128)}, u32[]{:S(2)}) %copy-start.1) | copy-done | bytes 65560
  3.1 0.0 copy-start.2
  3.1 0.8 %copy-done.2 = f32[8,8,256]{2,1,0:T(8,128)S(1)} copy-done((f32[8,8,256]{2,1,0:T(8,128)S(1)}, f32[8,8,256]{2,1,0:T(8,128)}, u32[]{:S(2)}) %copy-start.2) | copy-done | bytes 65560
  3.9 3.0 %x_sweep.1 = (f32[5,8,8,256]{3,2,1,0:T(8,128)S(1)}, f32[5,3,8,256]{3,2,1,0:T(8,128)S(1)}, f32[5,3,8,256]{3,2,1,0:T(8,128)S(1)}) custom-call(s32[6]{0:T(128)S(1)} %copy-done.3, s32[2]{0:T(128)S(1)} %pad_add_fusion.index, f32[8,8,256]{2,1,0:T(8,128)S(1)} %copy-done.1, f32[8,8,256]{2,1,0:T(8,128)S(1)} %copy-done.2, f32[3,8,8,256]{3,2,1,0:T(8,128)S(1)} %copy-done), custom_call_target="tpu_custom_call" | custom-call | tf_op jit(solution)/shard_map/x_sweep/pallas_call | solution.py:302
  6.9 2.3 %collective-permute-start = (f32[5,3,8,256]{3,2,1,0:T(8,128)S(1)}, f32[5,3,8,256]{3,2,1,0:T(8,128)S(1)}, u32[]{:S(2)}, u32[]{:S(2)}) collective-permute-start(f32[5,3,8,256]{3,2,1,0:T(8,128)S(1)} %get-tuple-element.10), channel_id=1, source_target_pairs={{1,2},{2,1},{3,4},{4,3},{5,6},{6,5},{7,8},{8,7},{9,10},{10,9},{11,... | collective-permute-start | bytes 368648 | tf_op jit(solution)/shard_map/ppermute | solution.py:277
  9.1 3.2 %collective-permute-start.1 = (f32[5,3,8,256]{3,2,1,0:T(8,128)S(1)}, f32[5,3,8,256]{3,2,1,0:T(8,128)S(1)}, u32[]{:S(2)}, u32[]{:S(2)}) collective-permute-start(f32[5,3,8,256]{3,2,1,0:T(8,128)S(1)} %get-tuple-element.11), channel_id=1, source_target_pairs={{0,1},{1,0},{2,3},{3,2},{4,5},{5,4},{6,7},{7,6},{8,9},{9,8},{10,11... | collective-permute-start | bytes 368648 | tf_op jit(solution)/shard_map/ppermute | solution.py:277
  12.3 12.9 %collective-permute-done.first = f32[5,3,8,256]{3,2,1,0:T(8,128)S(1)} collective-permute-done((f32[5,3,8,256]{3,2,1,0:T(8,128)S(1)}, f32[5,3,8,256]{3,2,1,0:T(8,128)S(1)}, u32[]{:S(2)}, u32[]{:S(2)}) %collective-permute-start) | collective-permute-done | bytes 122912 | tf_op jit(solution)/shard_map/ppermute | solution.py:277
  25.2 0.0 collective-permute-done.1.second
  25.2 1.5 %y_sweep.1 = (f32[5,8,8,256]{3,2,1,0:T(8,128)S(1)}, f32[5,3,8,256]{3,2,1,0:T(8,128)S(1)}, f32[5,3,8,256]{3,2,1,0:T(8,128)S(1)}) custom-call(s32[6]{0:T(128)S(1)} %copy-done.3, s32[2]{0:T(128)S(1)} %pad_add_fusion.index, f32[5,8,8,256]{3,2,1,0:T(8,128)S(1)} %get-tuple-element.9.main, f32[5,3,8,256]{3,2,1,0:T(8,128)S(1)} %collective-permute-done.first, ...), custom_call_target="tpu_custom_call" | custom-call | tf_op jit(solution)/shard_map/y_sweep/pallas_call | solution.py:317
  26.7 8.0 %collective-permute-start.2 = (f32[5,3,8,256]{3,2,1,0:T(8,128)S(1)}, f32[5,3,8,256]{3,2,1,0:T(8,128)S(1)}, u32[]{:S(2)}, u32[]{:S(2)}) collective-permute-start(f32[5,3,8,256]{3,2,1,0:T(8,128)S(1)} %get-tuple-element.13), channel_id=1, source_target_pairs={{16,32},{32,16},{48,64},{64,48},{80,96},{96,80},{112,128},{128,112... | collective-permute-start | bytes 368648 | tf_op jit(solution)/shard_map/ppermute | solution.py:277
  34.7 1.9 %collective-permute-start.3 = (f32[5,3,8,256]{3,2,1,0:T(8,128)S(1)}, f32[5,3,8,256]{3,2,1,0:T(8,128)S(1)}, u32[]{:S(2)}, u32[]{:S(2)}) collective-permute-start(f32[5,3,8,256]{3,2,1,0:T(8,128)S(1)} %get-tuple-element.14), channel_id=1, source_target_pairs={{0,16},{16,0},{32,48},{48,32},{64,80},{80,64},{96,112},{112,96},{1... | collective-permute-start | bytes 368648 | tf_op jit(solution)/shard_map/ppermute | solution.py:277
  36.6 0.9 %collective-permute-done.2.first = f32[5,3,8,256]{3,2,1,0:T(8,128)S(1)} collective-permute-done((f32[5,3,8,256]{3,2,1,0:T(8,128)S(1)}, f32[5,3,8,256]{3,2,1,0:T(8,128)S(1)}, u32[]{:S(2)}, u32[]{:S(2)}) %collective-permute-start.2) | collective-permute-done | bytes 122912 | tf_op jit(solution)/shard_map/ppermute | solution.py:277
  37.5 3.9 %collective-permute-done.3.second = f32[5,3,8,256]{3,2,1,0:T(8,128)S(1)} collective-permute-done((f32[5,3,8,256]{3,2,1,0:T(8,128)S(1)}, f32[5,3,8,256]{3,2,1,0:T(8,128)S(1)}, u32[]{:S(2)}, u32[]{:S(2)}) %collective-permute-start.3) | collective-permute-done | bytes 122912 | tf_op jit(solution)/shard_map/ppermute | solution.py:277
  41.5 2.2 %z_sweep.1 = (f32[8,8,256]{2,1,0:T(8,128)}, f32[8,8,256]{2,1,0:T(8,128)}, f32[3,8,8,256]{3,2,1,0:T(8,128)}) custom-call(s32[6]{0:T(128)S(1)} %copy-done.3, s32[2]{0:T(128)S(1)} %pad_add_fusion.index, f32[5,8,8,256]{3,2,1,0:T(8,128)S(1)} %get-tuple-element.12.main, f32[5,3,8,256]{3,2,1,0:T(8,128)S(1)} %collective-permute-done.2.first, ...), custom_call_target="tpu_custom_call" | custom-call | tf_op jit(solution)/shard_map/z_sweep/pallas_call | solution.py:328
Async XLA Ops:
  0.6 0.7 %copy-start.3 = (s32[6]{0:T(128)S(1)}, s32[6]{0:T(128)}, u32[]{:S(2)}) copy-start(s32[6]{0:T(128)} %flags.5) | copy-start | bytes 76
  1.3 0.9 %copy-start = (f32[3,8,8,256]{3,2,1,0:T(8,128)S(1)}, f32[3,8,8,256]{3,2,1,0:T(8,128)}, u32[]{:S(2)}) copy-start(f32[3,8,8,256]{3,2,1,0:T(8,128)} %vel.1) | copy-start | bytes 589828
  2.2 0.8 %copy-start.1 = (f32[8,8,256]{2,1,0:T(8,128)S(1)}, f32[8,8,256]{2,1,0:T(8,128)}, u32[]{:S(2)}) copy-start(f32[8,8,256]{2,1,0:T(8,128)} %dens.1) | copy-start | bytes 196612
  3.1 0.8 %copy-start.2 = (f32[8,8,256]{2,1,0:T(8,128)S(1)}, f32[8,8,256]{2,1,0:T(8,128)}, u32[]{:S(2)}) copy-start(f32[8,8,256]{2,1,0:T(8,128)} %press.1) | copy-start | bytes 196612
  6.9 18.3 %collective-permute-start = (f32[5,3,8,256]{3,2,1,0:T(8,128)S(1)}, f32[5,3,8,256]{3,2,1,0:T(8,128)S(1)}, u32[]{:S(2)}, u32[]{:S(2)}) collective-permute-start(f32[5,3,8,256]{3,2,1,0:T(8,128)S(1)} %get-tuple-element.10), channel_id=1, source_target_pairs={{1,2},{2,1},{3,4},{4,3},{5,6},{6,5},{7,8},{8,7},{9,10},{10,9},{11,... | collective-permute-start | bytes 368648 | tf_op jit(solution)/shard_map/ppermute | solution.py:277
  9.1 16.1 %collective-permute-start.1 = (f32[5,3,8,256]{3,2,1,0:T(8,128)S(1)}, f32[5,3,8,256]{3,2,1,0:T(8,128)S(1)}, u32[]{:S(2)}, u32[]{:S(2)}) collective-permute-start(f32[5,3,8,256]{3,2,1,0:T(8,128)S(1)} %get-tuple-element.11), channel_id=1, source_target_pairs={{0,1},{1,0},{2,3},{3,2},{4,5},{5,4},{6,7},{7,6},{8,9},{9,8},{10,11... | collective-permute-start | bytes 368648 | tf_op jit(solution)/shard_map/ppermute | solution.py:277
  26.7 10.9 %collective-permute-start.2 = (f32[5,3,8,256]{3,2,1,0:T(8,128)S(1)}, f32[5,3,8,256]{3,2,1,0:T(8,128)S(1)}, u32[]{:S(2)}, u32[]{:S(2)}) collective-permute-start(f32[5,3,8,256]{3,2,1,0:T(8,128)S(1)} %get-tuple-element.13), channel_id=1, source_target_pairs={{16,32},{32,16},{48,64},{64,48},{80,96},{96,80},{112,128},{128,112... | collective-permute-start | bytes 368648 | tf_op jit(solution)/shard_map/ppermute | solution.py:277
  34.7 6.8 %collective-permute-start.3 = (f32[5,3,8,256]{3,2,1,0:T(8,128)S(1)}, f32[5,3,8,256]{3,2,1,0:T(8,128)S(1)}, u32[]{:S(2)}, u32[]{:S(2)}) collective-permute-start(f32[5,3,8,256]{3,2,1,0:T(8,128)S(1)} %get-tuple-element.14), channel_id=1, source_target_pairs={{0,16},{16,0},{32,48},{48,32},{64,80},{80,64},{96,112},{112,96},{1... | collective-permute-start | bytes 368648 | tf_op jit(solution)/shard_map/ppermute | solution.py:277

commit v2 on v1

--- a/solution.py
+++ b/solution.py
@@ -69,6 +69,25 @@
     return (mass, (energy + star) * speed, mass * speed + star, mass * s, mass * t)
 
 
+def wall_flux(state, sign):
+    rho, p, u, s, t = state
+    inv = lax.rsqrt(GAMMA * (p * rho))
+    image = sign * u
+    jump = image - u
+    floor = STAR_FRAC * p
+    star = jnp.maximum(p - 0.5 * jump / inv, floor)
+    slope = RATIO_G / p
+    for _ in range(RIEMANN_ITERS):
+        root = lax.rsqrt((1.0 - RATIO_G) + slope * star)
+        scaled = inv * root
+        twice_f = 2.0 * (star - p) * scaled
+        star = jnp.maximum(star - (jump + twice_f) / (scaled * (1.0 + root * root)), floor)
+    speed = 0.5 * (u + image)
+    mass = rho * speed
+    energy = p * (1.0 / (GAMMA - 1.0)) + 0.5 * rho * (speed * speed + s * s + t * t)
+    return (mass, (energy + star) * speed, mass * speed + star, mass * s, mass * t)
+
+
 def advance(cell, flux_low, flux_high):
     rho, p, u, s, t = cell
     change = [COURANT * (high - low) for low, high in zip(flux_low, flux_high)]
@@ -91,20 +110,25 @@
 
 
 def x_kernel(
-    flags, index, dens, press, vel, main, first, second, left, right, turn
+    bounds, dens, press, vel, main, first, second, held, flags, sems, left, right, last, turn
 ):
     planes, rows, cells = dens.shape
+    copies = [pltpu.make_async_copy(bounds, flags, sems.at[5])]
+    for f, source in enumerate((dens, press, vel.at[0], vel.at[1], vel.at[2])):
+        copies.append(pltpu.make_async_copy(source, held.at[f], sems.at[f]))
+    for copy in copies:
+        copy.start()
+    for copy in copies:
+        copy.wait()
     pair = 2
     half = cells // LANES
     lane = lax.broadcasted_iota(jnp.int32, (pair * rows, cells), 1)
-    short = lax.broadcasted_iota(jnp.int32, (rows, LANES), 1)
+    end = lax.broadcasted_iota(jnp.int32, (pair * rows, LANES), 1) == LANES - 1
     sign_low, sign_high = sign_of(flags[0]), sign_of(flags[1])
 
     def load(field, start):
-        ref = (dens, press, vel.at[0], vel.at[1], vel.at[2])[field]
-        return ref[start : start + pair].reshape(pair * rows, cells)
-
-    edge = [jnp.zeros((rows, LANES), jnp.float32) for _ in range(5)]
+        return held[field, start : start + pair].reshape(pair * rows, cells)
+
     for start in range(0, planes, pair):
         block = slice(start * rows, (start + pair) * rows)
         for field in range(5):
@@ -121,25 +145,18 @@
             west, east = cell_edges(cell, face, face_next)
             left[field, block, :] = jnp.where(lane == 0, low * west, pltpu.roll(east, 1, 1))
             right[field, block, :] = west
-            for k in range(pair):
-                z = start + k
-                last = east[k * rows : (k + 1) * rows, cells - LANES :]
-                edge[field] = jnp.where(short == z, pltpu.roll(last, z + 1, 1), edge[field])
-    wall = [jnp.where(short < planes, e, 1.0) for e in edge]
-    wall_flux = godunov(wall, [w * sign_high if f == 2 else w for f, w in enumerate(wall)])
+            last[field, block, :] = east[:, cells - LANES :]
 
     for start in range(0, planes, pair):
         block = slice(start * rows, (start + pair) * rows)
         flux = godunov(
             [left[f, block, :] for f in range(5)], [right[f, block, :] for f in range(5)]
         )
+        upper = wall_flux([last[f, block, :] for f in range(5)], sign_high)
         after = []
         for f in range(5):
             rolled = pltpu.roll(flux[f], cells - 1, 1)
-            end = jnp.concatenate(
-                [pltpu.roll(wall_flux[f], LANES - 1 - start - k, 1) for k in range(pair)], axis=0
-            )
-            tail = jnp.where(short_pair(short, pair) == LANES - 1, end, rolled[:, cells - LANES :])
+            tail = jnp.where(end, upper[f], rolled[:, cells - LANES :])
             after.append(jnp.concatenate([rolled[:, : cells - LANES], tail], axis=1))
         new = advance([load(f, start) for f in range(5)], flux, after)
         for f in range(5):
@@ -147,11 +164,7 @@
                 base = ((f * half + h) * planes + start) * rows
                 turn[base : base + pair * rows, :] = new[f][:, h * LANES : (h + 1) * LANES]
     turn_over(turn, main, half)
-    edge_blocks(index[0], main, first, second)
-
-
-def short_pair(short, pair):
-    return jnp.concatenate([short] * pair, axis=0)
+    edge_blocks("row", main, first, second)
 
 
 def turn_over(turn, main, half):
@@ -163,28 +176,44 @@
                 main[f, j, :, h * LANES : (h + 1) * LANES] = turn[pl.ds(base + j, inner, stride=outer), :]
 
 
-def edge_blocks(place, main, first, second):
+RING = 4
+ROW_LATE = (3, 7)
+
+
+def ring_in(rings):
+    ring = lax.axis_index("gz") // RING
+    return functools.reduce(jnp.logical_or, [ring == k for k in rings], ring < 0)
+
+
+def upper_first(axis):
+    if axis == "gz":
+        return lax.rem(lax.axis_index("gz"), 2) == 0
+    return lax.rem(lax.axis_index("row"), 2) == jnp.where(ring_in(ROW_LATE), 0, 1)
+
+
+def edge_blocks(axis, main, first, second):
     outer = main.shape[1]
-    odd = lax.rem(place, 2) == 1
-    start_first = jnp.where(odd, outer - WIDTH, 0)
-    start_second = jnp.where(odd, 0, outer - WIDTH)
+    upper = upper_first(axis)
+    start_first = jnp.where(upper, outer - WIDTH, 0)
+    start_second = jnp.where(upper, 0, outer - WIDTH)
     for f in range(5):
         for k in range(WIDTH):
             first[f, k] = main[f, start_first + k]
             second[f, k] = main[f, start_second + k]
 
 
-def sweep_outer(place, count, flag_low, flag_high, normal, main, first, second, ghost, left, right, flux, store):
+def sweep_outer(axis, faces, bounds, flags, normal, main, first, second, ghost, left, right, flux, store):
     outer, rows, cells = main.shape[1:]
     half = cells // LANES
-    odd = lax.rem(place, 2) == 1
-
-    @pl.when(odd)
+    place, count = lax.axis_index(axis), lax.axis_size(axis)
+    upper = upper_first(axis)
+
+    @pl.when(upper)
     def _():
         ghost[:, :WIDTH] = second[...]
         ghost[:, WIDTH:] = first[...]
 
-    @pl.when(jnp.logical_not(odd))
+    @pl.when(jnp.logical_not(upper))
     def _():
         ghost[:, :WIDTH] = first[...]
         ghost[:, WIDTH:] = second[...]
@@ -197,11 +226,13 @@
 
     @pl.when(place == 0)
     def _():
-        wall(lambda k: WIDTH - 1 - k, 0, 1, flag_low)
+        pltpu.sync_copy(bounds, flags)
+        wall(lambda k: WIDTH - 1 - k, 0, 1, flags[faces])
 
     @pl.when(place == count - 1)
     def _():
-        wall(lambda k: WIDTH + k, outer - 1, -1, flag_high)
+        pltpu.sync_copy(bounds, flags)
+        wall(lambda k: WIDTH + k, outer - 1, -1, flags[faces + 1])
 
     order = field_order(normal)
     for f in range(5):
@@ -245,7 +276,7 @@
         store(i, {f: new[k] for k, f in enumerate(order)})
 
 
-def y_kernel(flags, index, main, first, second, out, out_first, out_second, ghost, left, right, flux, turn, *, count):
+def y_kernel(bounds, main, first, second, out, out_first, out_second, flags, ghost, left, right, flux, turn):
     outer, rows, cells = main.shape[1:]
     half = cells // LANES
 
@@ -255,34 +286,52 @@
                 base = ((f * half + h) * outer + i) * rows
                 turn[base : base + rows, :] = new[f][:, h * LANES : (h + 1) * LANES]
 
-    sweep_outer(index[0], count, flags[2], flags[3], 3, main, first, second, ghost, left, right, flux, store)
+    sweep_outer("row", 2, bounds, flags, 3, main, first, second, ghost, left, right, flux, store)
     turn_over(turn, out, half)
-    edge_blocks(index[1], out, out_first, out_second)
-
-
-def z_kernel(flags, index, main, first, second, dens, press, vel, ghost, left, right, flux, *, count):
+    edge_blocks("gz", out, out_first, out_second)
+
+
+def z_kernel(bounds, main, first, second, dens, press, vel, flags, ghost, left, right, flux):
     def store(i, new):
         dens[i] = new[0]
         press[i] = new[1]
         for v in range(3):
             vel[v, i] = new[2 + v]
 
-    sweep_outer(index[1], count, flags[4], flags[5], 4, main, first, second, ghost, left, right, flux, store)
-
-
-def exchange(block, axis, start):
+    sweep_outer("gz", 4, bounds, flags, 4, main, first, second, ghost, left, right, flux, store)
+
+
+def swap(block, places):
+    rows = lax.axis_size("row")
     pairs = []
-    for i in range(start, lax.axis_size(axis) - 1, 2):
-        pairs += [(i, i + 1), (i + 1, i)]
-    return lax.ppermute(block, axis, pairs)
+    for (g, r), (h, q) in places:
+        pairs += [(g * rows + r, h * rows + q), (h * rows + q, g * rows + r)]
+    return lax.ppermute(block, ("gz", "row"), pairs)
+
+
+def row_swap(block, turn):
+    places = []
+    for g in range(lax.axis_size("gz")):
+        start = turn if g // RING in ROW_LATE else 1 - turn
+        places += [((g, r), (g, r + 1)) for r in range(start, lax.axis_size("row") - 1, 2)]
+    return swap(block, places)
+
+
+def gz_swap(block, turn):
+    places = [
+        ((g, r), (g + 1, r))
+        for g in range(turn, lax.axis_size("gz") - 1, 2)
+        for r in range(lax.axis_size("row"))
+    ]
+    return swap(block, places)
 
 
 def on_device(density, pressure, velocity, boundary):
     planes, rows, cells = density.shape
     half = cells // LANES
     f32 = jnp.float32
-    place = jnp.stack([lax.axis_index("row"), lax.axis_index("gz")]).astype(jnp.int32)
-    smem = pl.BlockSpec(memory_space=pltpu.SMEM)
+    hbm = pl.BlockSpec(memory_space=pltpu.HBM)
+    flags = pltpu.SMEM((6,), jnp.int32)
     vmem = pl.BlockSpec(memory_space=pltpu.VMEM)
     params = pltpu.CompilerParams(vmem_limit_bytes=32 << 20)
     by_y = jax.ShapeDtypeStruct((5, rows, planes, cells), f32)
@@ -293,6 +342,7 @@
 
     def work(outer, inner):
         return [
+            flags,
             pltpu.VMEM((5, 2 * WIDTH, inner, cells), f32),
             pltpu.VMEM((5, outer + 1, inner, cells), f32),
             pltpu.VMEM((5, outer + 1, inner, cells), f32),
@@ -302,42 +352,46 @@
     main, first, second = pl.pallas_call(
         x_kernel,
         out_shape=(by_y, y_edge, y_edge),
-        in_specs=[smem, smem, vmem, vmem, vmem],
+        in_specs=[hbm, hbm, hbm, hbm],
         out_specs=(vmem, vmem, vmem),
         scratch_shapes=[
+            pltpu.VMEM((5, planes, rows, cells), f32),
+            flags,
+            pltpu.SemaphoreType.DMA((6,)),
             pltpu.VMEM((5, planes * rows, cells), f32),
             pltpu.VMEM((5, planes * rows, cells), f32),
+            pltpu.VMEM((5, planes * rows, LANES), f32),
             turn,
         ],
         compiler_params=params,
         name="x_sweep",
-    )(boundary, place, density, pressure, velocity)
-    first = exchange(first, "row", 1)
-    second = exchange(second, "row", 0)
+    )(*(pltpu.with_memory_space_constraint(a, pltpu.HBM) for a in (boundary, density, pressure, velocity)))
+    first = row_swap(first, 0)
+    second = row_swap(second, 1)
     main, first, second = pl.pallas_call(
-        functools.partial(y_kernel, count=lax.axis_size("row")),
+        y_kernel,
         out_shape=(by_z, z_edge, z_edge),
-        in_specs=[smem, smem, vmem, vmem, vmem],
+        in_specs=[hbm, vmem, vmem, vmem],
         out_specs=(vmem, vmem, vmem),
         scratch_shapes=work(rows, planes) + [turn],
         compiler_params=params,
         name="y_sweep",
-    )(boundary, place, main, first, second)
-    first = exchange(first, "gz", 1)
-    second = exchange(second, "gz", 0)
+    )(boundary, main, first, second)
+    first = gz_swap(first, 0)
+    second = gz_swap(second, 1)
     return pl.pallas_call(
-        functools.partial(z_kernel, count=lax.axis_size("gz")),
+        z_kernel,
         out_shape=(
             jax.ShapeDtypeStruct(density.shape, f32),
             jax.ShapeDtypeStruct(pressure.shape, f32),
             jax.ShapeDtypeStruct(velocity.shape, f32),
         ),
-        in_specs=[smem, smem, vmem, vmem, vmem],
+        in_specs=[hbm, vmem, vmem, vmem],
         out_specs=(vmem, vmem, vmem),
         scratch_shapes=work(planes, rows),
         compiler_params=params,
         name="z_sweep",
-    )(boundary, place, main, first, second)
+    )(boundary, main, first, second)
 
 
 def solution(mesh):

time: 43.9 us -> 37.9 us (0.86)
  the two profiles are of different devices: /device:TPU:320 before, /device:TPU:376 now
where the time goes in v2:
time: 37.9 us; the launch traced here: 37.7 us
  waiting for transfers between devices  21.6 us (57%)
  starting transfers between devices  10.3 us (27%)
  Pallas kernels  5.04 us (13%)
  between operations  0.69 us (2%)
    ppermute x4, waiting for transfers between devices, swap(): return lax.ppermute(block, ('gz', 'row'), pairs)  21.6 us
    ppermute x4, starting transfers between devices, swap(): return lax.ppermute(block, ('gz', 'row'), pairs)  10.3 us
    pallas_call x1, Pallas kernels, on_device(): pl.pallas_call(x_kernel, out_shape=(by_y, y_edge, y_edge), in_specs=[hbm,...  2.52 us
    pallas_call x1, Pallas kernels, on_device(): pl.pallas_call(z_kernel, out_shape=(jax.ShapeDtypeStruct(density.shape, f...  1.59 us
    pallas_call x1, Pallas kernels, on_device(): pl.pallas_call(y_kernel, out_shape=(by_z, z_edge, z_edge), in_specs=[hbm,...  0.92 us
  transfers between devices with their start and end apart: 4, of which 3 were waited for; matrix products, arithmetic and copies ran while one was open for 0% of the time, Pallas kernels for 0%

profile of v2, /device:TPU:376, one launch (start us, length us, event | category | flops | bytes accessed | tf_op | source)
XLA Modules:
  0.0 37.7 jit_solution(5352832036911588594)
XLA Ops:
  0.6 2.5 %x_sweep.1 = (f32[5,8,8,256]{3,2,1,0:T(8,128)S(1)}, f32[5,3,8,256]{3,2,1,0:T(8,128)S(1)}, f32[5,3,8,256]{3,2,1,0:T(8,128)S(1)}) custom-call(s32[6]{0:T(128)} %bounds.5, f32[8,8,256]{2,1,0:T(8,128)} %dens.1, f32[8,8,256]{2,1,0:T(8,128)} %press.1, f32[3,8,8,256]{3,2,1,0:T(8,128)} %vel.1), custom_call_target="tpu_custom_call" | custom-call | tf_op jit(solution)/shard_map/x_sweep/pallas_call | solution.py:352
  3.2 1.9 %collective-permute-start = (f32[5,3,8,256]{3,2,1,0:T(8,128)S(1)}, f32[5,3,8,256]{3,2,1,0:T(8,128)S(1)}, u32[]{:S(2)}, u32[]{:S(2)}) collective-permute-start(f32[5,3,8,256]{3,2,1,0:T(8,128)S(1)} %get-tuple-element.10), channel_id=1, source_target_pairs={{1,2},{2,1},{3,4},{4,3},{5,6},{6,5},{7,8},{8,7},{9,10},{10,9},{11,... | collective-permute-start | bytes 368648 | tf_op jit(solution)/shard_map/ppermute | solution.py:309
  5.1 0.0 copy-start
  5.1 3.8 %collective-permute-start.1 = (f32[5,3,8,256]{3,2,1,0:T(8,128)S(1)}, f32[5,3,8,256]{3,2,1,0:T(8,128)S(1)}, u32[]{:S(2)}, u32[]{:S(2)}) collective-permute-start(f32[5,3,8,256]{3,2,1,0:T(8,128)S(1)} %get-tuple-element.11), channel_id=1, source_target_pairs={{0,1},{1,0},{2,3},{3,2},{4,5},{5,4},{6,7},{7,6},{8,9},{9,8},{10,11... | collective-permute-start | bytes 368648 | tf_op jit(solution)/shard_map/ppermute | solution.py:309
  8.9 0.0 collective-permute-done.first
  8.9 13.5 %collective-permute-done.1.second = f32[5,3,8,256]{3,2,1,0:T(8,128)S(1)} collective-permute-done((f32[5,3,8,256]{3,2,1,0:T(8,128)S(1)}, f32[5,3,8,256]{3,2,1,0:T(8,128)S(1)}, u32[]{:S(2)}, u32[]{:S(2)}) %collective-permute-start.1) | collective-permute-done | bytes 122912 | tf_op jit(solution)/shard_map/ppermute | solution.py:309
  22.4 0.0 copy-done
  22.4 0.9 %y_sweep.1 = (f32[5,8,8,256]{3,2,1,0:T(8,128)S(1)}, f32[5,3,8,256]{3,2,1,0:T(8,128)S(1)}, f32[5,3,8,256]{3,2,1,0:T(8,128)S(1)}) custom-call(s32[6]{0:T(128)S(1)} %copy-done, f32[5,8,8,256]{3,2,1,0:T(8,128)S(1)} %get-tuple-element.9.main, f32[5,3,8,256]{3,2,1,0:T(8,128)S(1)} %collective-permute-done.first, f32[5,3,8,256]{3,2,1,0:T(8,128)S(1)} %collective-permute-done.1.second), custom_call_target="tpu_custom_call" | custom-call | tf_op jit(solution)/shard_map/y_sweep/pallas_call | solution.py:371
  23.3 2.7 %collective-permute-start.2 = (f32[5,3,8,256]{3,2,1,0:T(8,128)S(1)}, f32[5,3,8,256]{3,2,1,0:T(8,128)S(1)}, u32[]{:S(2)}, u32[]{:S(2)}) collective-permute-start(f32[5,3,8,256]{3,2,1,0:T(8,128)S(1)} %get-tuple-element.13), channel_id=1, source_target_pairs={{0,16},{16,0},{1,17},{17,1},{2,18},{18,2},{3,19},{19,3},{4,20},{20... | collective-permute-start | bytes 368648 | tf_op jit(solution)/shard_map/ppermute | solution.py:309
  26.0 1.9 %collective-permute-start.3 = (f32[5,3,8,256]{3,2,1,0:T(8,128)S(1)}, f32[5,3,8,256]{3,2,1,0:T(8,128)S(1)}, u32[]{:S(2)}, u32[]{:S(2)}) collective-permute-start(f32[5,3,8,256]{3,2,1,0:T(8,128)S(1)} %get-tuple-element.14), channel_id=1, source_target_pairs={{16,32},{32,16},{17,33},{33,17},{18,34},{34,18},{19,35},{35,19},{2... | collective-permute-start | bytes 368648 | tf_op jit(solution)/shard_map/ppermute | solution.py:309
  27.9 2.2 %collective-permute-done.2.first = f32[5,3,8,256]{3,2,1,0:T(8,128)S(1)} collective-permute-done((f32[5,3,8,256]{3,2,1,0:T(8,128)S(1)}, f32[5,3,8,256]{3,2,1,0:T(8,128)S(1)}, u32[]{:S(2)}, u32[]{:S(2)}) %collective-permute-start.2) | collective-permute-done | bytes 122912 | tf_op jit(solution)/shard_map/ppermute | solution.py:309
  30.1 6.0 %collective-permute-done.3.second = f32[5,3,8,256]{3,2,1,0:T(8,128)S(1)} collective-permute-done((f32[5,3,8,256]{3,2,1,0:T(8,128)S(1)}, f32[5,3,8,256]{3,2,1,0:T(8,128)S(1)}, u32[]{:S(2)}, u32[]{:S(2)}) %collective-permute-start.3) | collective-permute-done | bytes 122912 | tf_op jit(solution)/shard_map/ppermute | solution.py:309
  36.1 1.6 %z_sweep.1 = (f32[8,8,256]{2,1,0:T(8,128)}, f32[8,8,256]{2,1,0:T(8,128)}, f32[3,8,8,256]{3,2,1,0:T(8,128)}) custom-call(s32[6]{0:T(128)S(1)} %copy-done, f32[5,8,8,256]{3,2,1,0:T(8,128)S(1)} %get-tuple-element.12.main, f32[5,3,8,256]{3,2,1,0:T(8,128)S(1)} %collective-permute-done.2.first, f32[5,3,8,256]{3,2,1,0:T(8,128)S(1)} %collective-permute-done.3.second), custom_call_target="tpu_custom_call" | custom-call | tf_op jit(solution)/shard_map/z_sweep/pallas_call | solution.py:382
Async XLA Ops:
  3.2 5.8 %collective-permute-start = (f32[5,3,8,256]{3,2,1,0:T(8,128)S(1)}, f32[5,3,8,256]{3,2,1,0:T(8,128)S(1)}, u32[]{:S(2)}, u32[]{:S(2)}) collective-permute-start(f32[5,3,8,256]{3,2,1,0:T(8,128)S(1)} %get-tuple-element.10), channel_id=1, source_target_pairs={{1,2},{2,1},{3,4},{4,3},{5,6},{6,5},{7,8},{8,7},{9,10},{10,9},{11,... | collective-permute-start | bytes 368648 | tf_op jit(solution)/shard_map/ppermute | solution.py:309
  5.1 17.3 %copy-start = (s32[6]{0:T(128)S(1)}, s32[6]{0:T(128)}, u32[]{:S(2)}) copy-start(s32[6]{0:T(128)} %bounds.5) | copy-start | bytes 76
  5.1 17.3 %collective-permute-start.1 = (f32[5,3,8,256]{3,2,1,0:T(8,128)S(1)}, f32[5,3,8,256]{3,2,1,0:T(8,128)S(1)}, u32[]{:S(2)}, u32[]{:S(2)}) collective-permute-start(f32[5,3,8,256]{3,2,1,0:T(8,128)S(1)} %get-tuple-element.11), channel_id=1, source_target_pairs={{0,1},{1,0},{2,3},{3,2},{4,5},{5,4},{6,7},{7,6},{8,9},{9,8},{10,11... | collective-permute-start | bytes 368648 | tf_op jit(solution)/shard_map/ppermute | solution.py:309
  23.3 6.8 %collective-permute-start.2 = (f32[5,3,8,256]{3,2,1,0:T(8,128)S(1)}, f32[5,3,8,256]{3,2,1,0:T(8,128)S(1)}, u32[]{:S(2)}, u32[]{:S(2)}) collective-permute-start(f32[5,3,8,256]{3,2,1,0:T(8,128)S(1)} %get-tuple-element.13), channel_id=1, source_target_pairs={{0,16},{16,0},{1,17},{17,1},{2,18},{18,2},{3,19},{19,3},{4,20},{20... | collective-permute-start | bytes 368648 | tf_op jit(solution)/shard_map/ppermute | solution.py:309
  26.0 10.1 %collective-permute-start.3 = (f32[5,3,8,256]{3,2,1,0:T(8,128)S(1)}, f32[5,3,8,256]{3,2,1,0:T(8,128)S(1)}, u32[]{:S(2)}, u32[]{:S(2)}) collective-permute-start(f32[5,3,8,256]{3,2,1,0:T(8,128)S(1)} %get-tuple-element.14), channel_id=1, source_target_pairs={{16,32},{32,16},{17,33},{33,17},{18,34},{34,18},{19,35},{35,19},{2... | collective-permute-start | bytes 368648 | tf_op jit(solution)/shard_map/ppermute | solution.py:309

commit v3 on v2

--- a/solution.py
+++ b/solution.py
@@ -120,7 +120,7 @@
         copy.start()
     for copy in copies:
         copy.wait()
-    pair = 2
+    pair = 4
     half = cells // LANES
     lane = lax.broadcasted_iota(jnp.int32, (pair * rows, cells), 1)
     end = lax.broadcasted_iota(jnp.int32, (pair * rows, LANES), 1) == LANES - 1
@@ -183,6 +183,10 @@
 def ring_in(rings):
     ring = lax.axis_index("gz") // RING
     return functools.reduce(jnp.logical_or, [ring == k for k in rings], ring < 0)
+
+
+def parity(axis):
+    return lax.rem(lax.axis_index(axis), 2)
 
 
 def upper_first(axis):
@@ -291,14 +295,101 @@
     edge_blocks("gz", out, out_first, out_second)
 
 
-def z_kernel(bounds, main, first, second, dens, press, vel, flags, ghost, left, right, flux):
-    def store(i, new):
-        dens[i] = new[0]
-        press[i] = new[1]
-        for v in range(3):
-            vel[v, i] = new[2 + v]
-
-    sweep_outer("gz", 4, bounds, flags, 4, main, first, second, ghost, left, right, flux, store)
+def part_faces(block, count, flux, shift, left, right, order):
+    cells = block.shape[-1]
+    for f in range(5):
+        for h in range(cells // LANES):
+            part = slice(h * LANES, (h + 1) * LANES)
+            value = [block[f, i, :, part] for i in range(count + 5)]
+            face = face_value(*value[:4])
+            for i in range(2, count + 3):
+                face_next = face_value(*value[i - 1 : i + 3])
+                west, east = cell_edges(value[i], face, face_next)
+                if i < count + 2:
+                    left[f, i - 2, :, part] = east
+                if i > 2:
+                    right[f, i - 3, :, part] = west
+                face = face_next
+    for start in range(0, count, WIDTH):
+        for h in range(cells // LANES):
+            part = slice(h * LANES, (h + 1) * LANES)
+            out = godunov(
+                [left[f, start : start + WIDTH, :, part] for f in order],
+                [right[f, start : start + WIDTH, :, part] for f in order],
+            )
+            for f in range(5):
+                flux[f, pl.ds(start + shift, WIDTH), :, part] = out[f]
+
+
+def part_cells(block, skip, count, flux, held, order):
+    for i in range(count):
+        new = advance(
+            [block[f, skip + i] for f in order], [flux[f, i] for f in range(5)], [flux[f, i + 1] for f in range(5)]
+        )
+        for k, f in enumerate(order):
+            held[f, i] = new[k]
+
+
+def leave(held, dens, press, vel, base, sems):
+    count = held.shape[1]
+    part = pl.ds(base, count)
+    copies = [
+        pltpu.make_async_copy(held.at[0], dens.at[part], sems.at[0]),
+        pltpu.make_async_copy(held.at[1], press.at[part], sems.at[1]),
+    ]
+    for v in range(3):
+        copies.append(pltpu.make_async_copy(held.at[2 + v], vel.at[v, part], sems.at[2 + v]))
+    for copy in copies:
+        copy.start()
+    for copy in copies:
+        copy.wait()
+
+
+def z_most_kernel(main, first, dens, press, vel, border, block, left, right, flux, held, sems):
+    outer = main.shape[1]
+    upper = parity("gz") == 0
+    order = field_order(4)
+    most = outer - WIDTH
+    block[:, pl.ds(jnp.where(upper, 0, WIDTH), outer)] = main[...]
+    block[:, pl.ds(jnp.where(upper, outer, 0), WIDTH)] = first[...]
+    part_faces(block, most + 1, flux, 0, left, right, order)
+    border[...] = flux[:, jnp.where(upper, 0, most)]
+    part_cells(block, WIDTH, most, flux, held, order)
+    leave(held, dens, press, vel, jnp.where(upper, WIDTH, 0), sems)
+
+
+def z_rest_kernel(
+    bounds, main, second, border, dens_in, press_in, vel_in, dens, press, vel, flags, block, left, right, flux, held, sems
+):
+    del dens_in, press_in, vel_in
+    outer = main.shape[1]
+    place, count = lax.axis_index("gz"), lax.axis_size("gz")
+    upper = lax.rem(place, 2) == 0
+    order = field_order(4)
+    near = outer - WIDTH
+    block[:, pl.ds(jnp.where(upper, WIDTH, 0), near)] = main[:, pl.ds(jnp.where(upper, 0, WIDTH), near)]
+    block[:, pl.ds(jnp.where(upper, 0, near), WIDTH)] = second[...]
+
+    def wall(slot, edge, step, flag):
+        for f in range(5):
+            sign = sign_of(flag) if f == 4 else 1.0
+            for k in range(WIDTH):
+                block[f, slot(k)] = jnp.where(flag == 1, sign * main[f, edge + step * k], main[f, edge])
+
+    @pl.when(place == 0)
+    def _():
+        pltpu.sync_copy(bounds, flags)
+        wall(lambda k: WIDTH - 1 - k, 0, 1, flags[4])
+
+    @pl.when(place == count - 1)
+    def _():
+        pltpu.sync_copy(bounds, flags)
+        wall(lambda k: near + k, outer - 1, -1, flags[5])
+
+    part_faces(block, WIDTH, flux, jnp.where(upper, 0, 1), left, right, order)
+    flux[:, jnp.where(upper, WIDTH, 0)] = border[...]
+    part_cells(block, jnp.where(upper, WIDTH, WIDTH - 1), WIDTH, flux, held, order)
+    leave(held, dens, press, vel, jnp.where(upper, 0, near), sems)
 
 
 def swap(block, places):
@@ -379,19 +470,42 @@
     )(boundary, main, first, second)
     first = gz_swap(first, 0)
     second = gz_swap(second, 1)
+    results = (
+        jax.ShapeDtypeStruct(density.shape, f32),
+        jax.ShapeDtypeStruct(pressure.shape, f32),
+        jax.ShapeDtypeStruct(velocity.shape, f32),
+    )
+
+    def z_work(faces, whole, done):
+        return [
+            pltpu.VMEM((5, whole, rows, cells), f32),
+            pltpu.VMEM((5, faces, rows, cells), f32),
+            pltpu.VMEM((5, faces, rows, cells), f32),
+            pltpu.VMEM((5, done + 1, rows, cells), f32),
+            pltpu.VMEM((5, done, rows, cells), f32),
+            pltpu.SemaphoreType.DMA((5,)),
+        ]
+
+    most = planes - WIDTH
+    *partial, border = pl.pallas_call(
+        z_most_kernel,
+        out_shape=results + (jax.ShapeDtypeStruct((5, rows, cells), f32),),
+        in_specs=[vmem, vmem],
+        out_specs=(hbm, hbm, hbm, vmem),
+        scratch_shapes=z_work(most + 1, planes + WIDTH, most),
+        compiler_params=params,
+        name="z_sweep_most",
+    )(main, first)
     return pl.pallas_call(
-        z_kernel,
-        out_shape=(
-            jax.ShapeDtypeStruct(density.shape, f32),
-            jax.ShapeDtypeStruct(pressure.shape, f32),
-            jax.ShapeDtypeStruct(velocity.shape, f32),
-        ),
-        in_specs=[hbm, vmem, vmem, vmem],
-        out_specs=(vmem, vmem, vmem),
-        scratch_shapes=work(planes, rows),
+        z_rest_kernel,
+        out_shape=results,
+        in_specs=[hbm, vmem, vmem, vmem, hbm, hbm, hbm],
+        out_specs=(hbm, hbm, hbm),
+        scratch_shapes=[flags] + z_work(WIDTH, planes, WIDTH),
+        input_output_aliases={4: 0, 5: 1, 6: 2},
         compiler_params=params,
-        name="z_sweep",
-    )(boundary, main, first, second)
+        name="z_sweep_rest",
+    )(boundary, main, second, border, *partial)
 
 
 def solution(mesh):

time: 37.9 us -> 37.3 us (0.984)
  waiting for transfers between devices: 21.6 us -> 20.3 us
  Pallas kernels: 5.04 us -> 5.74 us
    ppermute x4, waiting for transfers between devices: 21.6 us -> 20.3 us  [swap(): return lax.ppermute(block, ('gz', 'row'), pairs)]
    pallas_call x1 -> x2, Pallas kernels: 1.59 us -> 2.37 us  [the longest x1 1.34 us: on_device(): pl.pallas_call(z_most_kernel, out_shape=results + (jax.ShapeDtypeStruct((...]
  transfers between devices with their start and end apart: 4 -> 4, of which waited for: 3 -> 3; matrix products, arithmetic and copies ran while one was open for 0% -> 0% of each run, Pallas kernels for 0% -> 4%
where the time goes in v3:
time: 37.3 us; the launch traced here: 37 us
  waiting for transfers between devices  20.3 us (54%)
  starting transfers between devices  10.3 us (28%)
  Pallas kernels  5.74 us (15%)
  between operations  0.7 us (2%)
    ppermute x4, waiting for transfers between devices, swap(): return lax.ppermute(block, ('gz', 'row'), pairs)  20.3 us
    ppermute x4, starting transfers between devices, swap(): return lax.ppermute(block, ('gz', 'row'), pairs)  10.3 us
    pallas_call x1, Pallas kernels, on_device(): pl.pallas_call(x_kernel, out_shape=(by_y, y_edge, y_edge), in_specs=[hbm,...  2.44 us
    pallas_call x1, Pallas kernels, on_device(): pl.pallas_call(z_most_kernel, out_shape=results + (jax.ShapeDtypeStruct((...  1.34 us
    pallas_call x1, Pallas kernels, on_device(): pl.pallas_call(z_rest_kernel, out_shape=results, in_specs=[hbm, vmem, vme...  1.04 us
    pallas_call x1, Pallas kernels, on_device(): pl.pallas_call(y_kernel, out_shape=(by_z, z_edge, z_edge), in_specs=[hbm,...  0.92 us
  transfers between devices with their start and end apart: 4, of which 3 were waited for; matrix products, arithmetic and copies ran while one was open for 0% of the time, Pallas kernels for 4%

profile of v3, /device:TPU:376, one launch (start us, length us, event | category | flops | bytes accessed | tf_op | source)
XLA Modules:
  0.0 37.0 jit_solution(8284236782708964843)
XLA Ops:
  0.6 2.4 %x_sweep.1 = (f32[5,8,8,256]{3,2,1,0:T(8,128)S(1)}, f32[5,3,8,256]{3,2,1,0:T(8,128)S(1)}, f32[5,3,8,256]{3,2,1,0:T(8,128)S(1)}) custom-call(s32[6]{0:T(128)} %bounds.5, f32[8,8,256]{2,1,0:T(8,128)} %dens.1, f32[8,8,256]{2,1,0:T(8,128)} %press.1, f32[3,8,8,256]{3,2,1,0:T(8,128)} %vel.1), custom_call_target="tpu_custom_call" | custom-call | tf_op jit(solution)/shard_map/x_sweep/pallas_call | solution.py:443
  3.1 1.9 %collective-permute-start = (f32[5,3,8,256]{3,2,1,0:T(8,128)S(1)}, f32[5,3,8,256]{3,2,1,0:T(8,128)S(1)}, u32[]{:S(2)}, u32[]{:S(2)}) collective-permute-start(f32[5,3,8,256]{3,2,1,0:T(8,128)S(1)} %get-tuple-element.14), channel_id=1, source_target_pairs={{1,2},{2,1},{3,4},{4,3},{5,6},{6,5},{7,8},{8,7},{9,10},{10,9},{11,... | collective-permute-start | bytes 368648 | tf_op jit(solution)/shard_map/ppermute | solution.py:400
  5.0 0.0 copy-start
  5.0 3.8 %collective-permute-start.1 = (f32[5,3,8,256]{3,2,1,0:T(8,128)S(1)}, f32[5,3,8,256]{3,2,1,0:T(8,128)S(1)}, u32[]{:S(2)}, u32[]{:S(2)}) collective-permute-start(f32[5,3,8,256]{3,2,1,0:T(8,128)S(1)} %get-tuple-element.15), channel_id=1, source_target_pairs={{0,1},{1,0},{2,3},{3,2},{4,5},{5,4},{6,7},{7,6},{8,9},{9,8},{10,11... | collective-permute-start | bytes 368648 | tf_op jit(solution)/shard_map/ppermute | solution.py:400
  8.9 0.0 collective-permute-done.first
  8.9 13.5 %collective-permute-done.1.second = f32[5,3,8,256]{3,2,1,0:T(8,128)S(1)} collective-permute-done((f32[5,3,8,256]{3,2,1,0:T(8,128)S(1)}, f32[5,3,8,256]{3,2,1,0:T(8,128)S(1)}, u32[]{:S(2)}, u32[]{:S(2)}) %collective-permute-start.1) | collective-permute-done | bytes 122912 | tf_op jit(solution)/shard_map/ppermute | solution.py:400
  22.3 0.0 copy-done
  22.3 0.9 %y_sweep.1 = (f32[5,8,8,256]{3,2,1,0:T(8,128)S(1)}, f32[5,3,8,256]{3,2,1,0:T(8,128)S(1)}, f32[5,3,8,256]{3,2,1,0:T(8,128)S(1)}) custom-call(s32[6]{0:T(128)S(1)} %copy-done, f32[5,8,8,256]{3,2,1,0:T(8,128)S(1)} %get-tuple-element.13.main, f32[5,3,8,256]{3,2,1,0:T(8,128)S(1)} %collective-permute-done.first, f32[5,3,8,256]{3,2,1,0:T(8,128)S(1)} %collective-permute-done.1.second), custom_call_target="tpu_custom_call" | custom-call | tf_op jit(solution)/shard_map/y_sweep/pallas_call | solution.py:462
  23.3 2.7 %collective-permute-start.3 = (f32[5,3,8,256]{3,2,1,0:T(8,128)S(1)}, f32[5,3,8,256]{3,2,1,0:T(8,128)S(1)}, u32[]{:S(2)}, u32[]{:S(2)}) collective-permute-start(f32[5,3,8,256]{3,2,1,0:T(8,128)S(1)} %get-tuple-element.18), channel_id=1, source_target_pairs={{0,16},{16,0},{1,17},{17,1},{2,18},{18,2},{3,19},{19,3},{4,20},{20... | collective-permute-start | bytes 368648 | tf_op jit(solution)/shard_map/ppermute | solution.py:400
  25.9 1.9 %collective-permute-start.2 = (f32[5,3,8,256]{3,2,1,0:T(8,128)S(1)}, f32[5,3,8,256]{3,2,1,0:T(8,128)S(1)}, u32[]{:S(2)}, u32[]{:S(2)}) collective-permute-start(f32[5,3,8,256]{3,2,1,0:T(8,128)S(1)} %get-tuple-element.17), channel_id=1, source_target_pairs={{16,32},{32,16},{17,33},{33,17},{18,34},{34,18},{19,35},{35,19},{2... | collective-permute-start | bytes 368648 | tf_op jit(solution)/shard_map/ppermute | solution.py:400
  27.8 2.2 %collective-permute-done.3.first = f32[5,3,8,256]{3,2,1,0:T(8,128)S(1)} collective-permute-done((f32[5,3,8,256]{3,2,1,0:T(8,128)S(1)}, f32[5,3,8,256]{3,2,1,0:T(8,128)S(1)}, u32[]{:S(2)}, u32[]{:S(2)}) %collective-permute-start.3) | collective-permute-done | bytes 122912 | tf_op jit(solution)/shard_map/ppermute | solution.py:400
  30.0 1.3 %z_sweep_most.1 = (f32[8,8,256]{2,1,0:T(8,128)}, f32[8,8,256]{2,1,0:T(8,128)}, f32[3,8,8,256]{3,2,1,0:T(8,128)}, f32[5,8,256]{2,1,0:T(8,128)S(1)}) custom-call(f32[5,8,8,256]{3,2,1,0:T(8,128)S(1)} %get-tuple-element.16.main, f32[5,3,8,256]{3,2,1,0:T(8,128)S(1)} %collective-permute-done.3.first), custom_call_target="tpu_custom_call" | custom-call | tf_op jit(solution)/shard_map/z_sweep_most/pallas_call | solution.py:490
  31.4 4.6 %collective-permute-done.2.second = f32[5,3,8,256]{3,2,1,0:T(8,128)S(1)} collective-permute-done((f32[5,3,8,256]{3,2,1,0:T(8,128)S(1)}, f32[5,3,8,256]{3,2,1,0:T(8,128)S(1)}, u32[]{:S(2)}, u32[]{:S(2)}) %collective-permute-start.2) | collective-permute-done | bytes 122912 | tf_op jit(solution)/shard_map/ppermute | solution.py:400
  36.0 1.0 %z_sweep_rest.1 = (f32[8,8,256]{2,1,0:T(8,128)}, f32[8,8,256]{2,1,0:T(8,128)}, f32[3,8,8,256]{3,2,1,0:T(8,128)}) custom-call(s32[6]{0:T(128)S(1)} %copy-done, f32[5,8,8,256]{3,2,1,0:T(8,128)S(1)} %get-tuple-element.16.main, f32[5,3,8,256]{3,2,1,0:T(8,128)S(1)} %collective-permute-done.2.second, ...), custom_call_target="tpu_custom_call", output_to_operand_aliasing={{0}: (4, {}), {1}: (5, {}), {2}: (6, {})} | custom-call | tf_op jit(solution)/shard_map/z_sweep_rest/pallas_call | solution.py:499
Async XLA Ops:
  3.1 5.8 %collective-permute-start = (f32[5,3,8,256]{3,2,1,0:T(8,128)S(1)}, f32[5,3,8,256]{3,2,1,0:T(8,128)S(1)}, u32[]{:S(2)}, u32[]{:S(2)}) collective-permute-start(f32[5,3,8,256]{3,2,1,0:T(8,128)S(1)} %get-tuple-element.14), channel_id=1, source_target_pairs={{1,2},{2,1},{3,4},{4,3},{5,6},{6,5},{7,8},{8,7},{9,10},{10,9},{11,... | collective-permute-start | bytes 368648 | tf_op jit(solution)/shard_map/ppermute | solution.py:400
  5.0 17.3 %copy-start = (s32[6]{0:T(128)S(1)}, s32[6]{0:T(128)}, u32[]{:S(2)}) copy-start(s32[6]{0:T(128)} %bounds.5) | copy-start | bytes 76
  5.0 17.3 %collective-permute-start.1 = (f32[5,3,8,256]{3,2,1,0:T(8,128)S(1)}, f32[5,3,8,256]{3,2,1,0:T(8,128)S(1)}, u32[]{:S(2)}, u32[]{:S(2)}) collective-permute-start(f32[5,3,8,256]{3,2,1,0:T(8,128)S(1)} %get-tuple-element.15), channel_id=1, source_target_pairs={{0,1},{1,0},{2,3},{3,2},{4,5},{5,4},{6,7},{7,6},{8,9},{9,8},{10,11... | collective-permute-start | bytes 368648 | tf_op jit(solution)/shard_map/ppermute | solution.py:400
  23.3 6.8 %collective-permute-start.3 = (f32[5,3,8,256]{3,2,1,0:T(8,128)S(1)}, f32[5,3,8,256]{3,2,1,0:T(8,128)S(1)}, u32[]{:S(2)}, u32[]{:S(2)}) collective-permute-start(f32[5,3,8,256]{3,2,1,0:T(8,128)S(1)} %get-tuple-element.18), channel_id=1, source_target_pairs={{0,16},{16,0},{1,17},{17,1},{2,18},{18,2},{3,19},{19,3},{4,20},{20... | collective-permute-start | bytes 368648 | tf_op jit(solution)/shard_map/ppermute | solution.py:400
  25.9 10.1 %collective-permute-start.2 = (f32[5,3,8,256]{3,2,1,0:T(8,128)S(1)}, f32[5,3,8,256]{3,2,1,0:T(8,128)S(1)}, u32[]{:S(2)}, u32[]{:S(2)}) collective-permute-start(f32[5,3,8,256]{3,2,1,0:T(8,128)S(1)} %get-tuple-element.17), channel_id=1, source_target_pairs={{16,32},{32,16},{17,33},{33,17},{18,34},{34,18},{19,35},{35,19},{2... | collective-permute-start | bytes 368648 | tf_op jit(solution)/shard_map/ppermute | solution.py:400

commit v4 on v3

--- a/solution.py
+++ b/solution.py
@@ -204,95 +204,6 @@
         for k in range(WIDTH):
             first[f, k] = main[f, start_first + k]
             second[f, k] = main[f, start_second + k]
-
-
-def sweep_outer(axis, faces, bounds, flags, normal, main, first, second, ghost, left, right, flux, store):
-    outer, rows, cells = main.shape[1:]
-    half = cells // LANES
-    place, count = lax.axis_index(axis), lax.axis_size(axis)
-    upper = upper_first(axis)
-
-    @pl.when(upper)
-    def _():
-        ghost[:, :WIDTH] = second[...]
-        ghost[:, WIDTH:] = first[...]
-
-    @pl.when(jnp.logical_not(upper))
-    def _():
-        ghost[:, :WIDTH] = first[...]
-        ghost[:, WIDTH:] = second[...]
-
-    def wall(slot, edge, step, flag):
-        for f in range(5):
-            sign = sign_of(flag) if f == normal else 1.0
-            for k in range(WIDTH):
-                ghost[f, slot(k)] = jnp.where(flag == 1, sign * main[f, edge + step * k], main[f, edge])
-
-    @pl.when(place == 0)
-    def _():
-        pltpu.sync_copy(bounds, flags)
-        wall(lambda k: WIDTH - 1 - k, 0, 1, flags[faces])
-
-    @pl.when(place == count - 1)
-    def _():
-        pltpu.sync_copy(bounds, flags)
-        wall(lambda k: WIDTH + k, outer - 1, -1, flags[faces + 1])
-
-    order = field_order(normal)
-    for f in range(5):
-        for h in range(half):
-            part = slice(h * LANES, (h + 1) * LANES)
-
-            def cell(i):
-                if i < 0:
-                    return ghost[f, WIDTH + i, :, part]
-                if i >= outer:
-                    return ghost[f, WIDTH + i - outer, :, part]
-                return main[f, i, :, part]
-
-            value = {i: cell(i) for i in range(-WIDTH, outer + WIDTH)}
-            face = None
-            for i in range(-1, outer + 1):
-                if face is None:
-                    face = face_value(*(value[i + d] for d in (-2, -1, 0, 1)))
-                face_next = face_value(*(value[i + d] for d in (-1, 0, 1, 2)))
-                west, east = cell_edges(value[i], face, face_next)
-                if i < outer:
-                    left[f, i + 1, :, part] = east
-                if i >= 0:
-                    right[f, i, :, part] = west
-                face = face_next
-    chunk = 3
-    for start in range(0, outer + 1, chunk):
-        stop = min(start + chunk, outer + 1)
-        for h in range(half):
-            part = slice(h * LANES, (h + 1) * LANES)
-            out = godunov(
-                [left[f, start:stop, :, part] for f in order],
-                [right[f, start:stop, :, part] for f in order],
-            )
-            for f in range(5):
-                flux[f, start:stop, :, part] = out[f]
-    for i in range(outer):
-        new = advance(
-            [main[f, i] for f in order], [flux[f, i] for f in range(5)], [flux[f, i + 1] for f in range(5)]
-        )
-        store(i, {f: new[k] for k, f in enumerate(order)})
-
-
-def y_kernel(bounds, main, first, second, out, out_first, out_second, flags, ghost, left, right, flux, turn):
-    outer, rows, cells = main.shape[1:]
-    half = cells // LANES
-
-    def store(i, new):
-        for f in range(5):
-            for h in range(half):
-                base = ((f * half + h) * outer + i) * rows
-                turn[base : base + rows, :] = new[f][:, h * LANES : (h + 1) * LANES]
-
-    sweep_outer("row", 2, bounds, flags, 3, main, first, second, ghost, left, right, flux, store)
-    turn_over(turn, out, half)
-    edge_blocks("gz", out, out_first, out_second)
 
 
 def part_faces(block, count, flux, shift, left, right, order):
@@ -345,16 +256,85 @@
         copy.wait()
 
 
-def z_most_kernel(main, first, dens, press, vel, border, block, left, right, flux, held, sems):
+def walls(axis, faces, bounds, flags, normal, main, block, upper, low_slot, high_slot):
     outer = main.shape[1]
-    upper = parity("gz") == 0
-    order = field_order(4)
+    place, count = lax.axis_index(axis), lax.axis_size(axis)
+
+    def fill(slot, edge, step, flag):
+        for f in range(5):
+            sign = sign_of(flag) if f == normal else 1.0
+            for k in range(WIDTH):
+                block[f, slot(k)] = jnp.where(flag == 1, sign * main[f, edge + step * k], main[f, edge])
+
+    @pl.when(jnp.logical_and(place == 0, jnp.logical_not(upper)))
+    def _():
+        pltpu.sync_copy(bounds, flags)
+        fill(low_slot, 0, 1, flags[faces])
+
+    @pl.when(jnp.logical_and(place == count - 1, upper))
+    def _():
+        pltpu.sync_copy(bounds, flags)
+        fill(high_slot, outer - 1, -1, flags[faces + 1])
+
+
+def sweep_most(axis, faces, bounds, flags, normal, upper, main, first, border, block, left, right, flux, held):
+    outer = main.shape[1]
+    order = field_order(normal)
     most = outer - WIDTH
     block[:, pl.ds(jnp.where(upper, 0, WIDTH), outer)] = main[...]
     block[:, pl.ds(jnp.where(upper, outer, 0), WIDTH)] = first[...]
+    walls(axis, faces, bounds, flags, normal, main, block, upper, lambda k: WIDTH - 1 - k, lambda k: outer + k)
     part_faces(block, most + 1, flux, 0, left, right, order)
     border[...] = flux[:, jnp.where(upper, 0, most)]
     part_cells(block, WIDTH, most, flux, held, order)
+
+
+def sweep_rest(axis, faces, bounds, flags, normal, upper, main, second, border, block, left, right, flux, held):
+    outer = main.shape[1]
+    order = field_order(normal)
+    near = outer - WIDTH
+    block[:, pl.ds(jnp.where(upper, WIDTH, 0), near)] = main[:, pl.ds(jnp.where(upper, 0, WIDTH), near)]
+    block[:, pl.ds(jnp.where(upper, 0, near), WIDTH)] = second[...]
+    walls(
+        axis, faces, bounds, flags, normal, main, block, jnp.logical_not(upper),
+        lambda k: WIDTH - 1 - k, lambda k: near + k,
+    )
+    part_faces(block, WIDTH, flux, jnp.where(upper, 0, 1), left, right, order)
+    flux[:, jnp.where(upper, WIDTH, 0)] = border[...]
+    part_cells(block, jnp.where(upper, WIDTH, WIDTH - 1), WIDTH, flux, held, order)
+
+
+def y_most_kernel(bounds, main, first, held, border, flags, block, left, right, flux):
+    sweep_most("row", 2, bounds, flags, 3, upper_first("row"), main, first, border, block, left, right, flux, held)
+
+
+def y_rest_kernel(
+    bounds, main, second, border, done, out, out_first, out_second, flags, block, left, right, flux, held, turn
+):
+    outer, rows, cells = main.shape[1:]
+    half = cells // LANES
+    upper = upper_first("row")
+    near = outer - WIDTH
+    sweep_rest("row", 2, bounds, flags, 3, upper, main, second, border, block, left, right, flux, held)
+
+    def place_rows(source, at):
+        count = source.shape[1]
+        for f in range(5):
+            for h in range(half):
+                base = (f * half + h) * outer * rows + at * rows
+                for i in range(count):
+                    start = pl.multiple_of(base + i * rows, rows)
+                    turn[pl.ds(start, rows), :] = source[f, i, :, h * LANES : (h + 1) * LANES]
+
+    place_rows(done, jnp.where(upper, WIDTH, 0))
+    place_rows(held, jnp.where(upper, 0, near))
+    turn_over(turn, out, half)
+    edge_blocks("gz", out, out_first, out_second)
+
+
+def z_most_kernel(bounds, main, first, dens, press, vel, border, flags, block, left, right, flux, held, sems):
+    upper = upper_first("gz")
+    sweep_most("gz", 4, bounds, flags, 4, upper, main, first, border, block, left, right, flux, held)
     leave(held, dens, press, vel, jnp.where(upper, WIDTH, 0), sems)
 
 
@@ -362,34 +342,9 @@
     bounds, main, second, border, dens_in, press_in, vel_in, dens, press, vel, flags, block, left, right, flux, held, sems
 ):
     del dens_in, press_in, vel_in
-    outer = main.shape[1]
-    place, count = lax.axis_index("gz"), lax.axis_size("gz")
-    upper = lax.rem(place, 2) == 0
-    order = field_order(4)
-    near = outer - WIDTH
-    block[:, pl.ds(jnp.where(upper, WIDTH, 0), near)] = main[:, pl.ds(jnp.where(upper, 0, WIDTH), near)]
-    block[:, pl.ds(jnp.where(upper, 0, near), WIDTH)] = second[...]
-
-    def wall(slot, edge, step, flag):
-        for f in range(5):
-            sign = sign_of(flag) if f == 4 else 1.0
-            for k in range(WIDTH):
-                block[f, slot(k)] = jnp.where(flag == 1, sign * main[f, edge + step * k], main[f, edge])
-
-    @pl.when(place == 0)
-    def _():
-        pltpu.sync_copy(bounds, flags)
-        wall(lambda k: WIDTH - 1 - k, 0, 1, flags[4])
-
-    @pl.when(place == count - 1)
-    def _():
-        pltpu.sync_copy(bounds, flags)
-        wall(lambda k: near + k, outer - 1, -1, flags[5])
-
-    part_faces(block, WIDTH, flux, jnp.where(upper, 0, 1), left, right, order)
-    flux[:, jnp.where(upper, WIDTH, 0)] = border[...]
-    part_cells(block, jnp.where(upper, WIDTH, WIDTH - 1), WIDTH, flux, held, order)
-    leave(held, dens, press, vel, jnp.where(upper, 0, near), sems)
+    upper = upper_first("gz")
+    sweep_rest("gz", 4, bounds, flags, 4, upper, main, second, border, block, left, right, flux, held)
+    leave(held, dens, press, vel, jnp.where(upper, 0, main.shape[1] - WIDTH), sems)
 
 
 def swap(block, places):
@@ -431,13 +386,13 @@
     z_edge = jax.ShapeDtypeStruct((5, WIDTH, rows, cells), f32)
     turn = pltpu.VMEM((5 * half * planes * rows, LANES), f32)
 
-    def work(outer, inner):
+    def part_work(inner, faces, whole, done):
         return [
             flags,
-            pltpu.VMEM((5, 2 * WIDTH, inner, cells), f32),
-            pltpu.VMEM((5, outer + 1, inner, cells), f32),
-            pltpu.VMEM((5, outer + 1, inner, cells), f32),
-            pltpu.VMEM((5, outer + 1, inner, cells), f32),
+            pltpu.VMEM((5, whole, inner, cells), f32),
+            pltpu.VMEM((5, faces, inner, cells), f32),
+            pltpu.VMEM((5, faces, inner, cells), f32),
+            pltpu.VMEM((5, done + 1, inner, cells), f32),
         ]
 
     main, first, second = pl.pallas_call(
@@ -459,15 +414,29 @@
     )(*(pltpu.with_memory_space_constraint(a, pltpu.HBM) for a in (boundary, density, pressure, velocity)))
     first = row_swap(first, 0)
     second = row_swap(second, 1)
+    most = rows - WIDTH
+    done, border = pl.pallas_call(
+        y_most_kernel,
+        out_shape=(
+            jax.ShapeDtypeStruct((5, most, planes, cells), f32),
+            jax.ShapeDtypeStruct((5, planes, cells), f32),
+        ),
+        in_specs=[hbm, vmem, vmem],
+        out_specs=(vmem, vmem),
+        scratch_shapes=part_work(planes, most + 1, rows + WIDTH, most),
+        compiler_params=params,
+        name="y_sweep_most",
+    )(boundary, main, first)
     main, first, second = pl.pallas_call(
-        y_kernel,
+        y_rest_kernel,
         out_shape=(by_z, z_edge, z_edge),
-        in_specs=[hbm, vmem, vmem, vmem],
+        in_specs=[hbm, vmem, vmem, vmem, vmem],
         out_specs=(vmem, vmem, vmem),
-        scratch_shapes=work(rows, planes) + [turn],
+        scratch_shapes=part_work(planes, WIDTH, rows, WIDTH)
+        + [pltpu.VMEM((5, WIDTH, planes, cells), f32), turn],
         compiler_params=params,
-        name="y_sweep",
-    )(boundary, main, first, second)
+        name="y_sweep_rest",
+    )(boundary, main, second, border, done)
     first = gz_swap(first, 0)
     second = gz_swap(second, 1)
     results = (
@@ -477,11 +446,7 @@
     )
 
     def z_work(faces, whole, done):
-        return [
-            pltpu.VMEM((5, whole, rows, cells), f32),
-            pltpu.VMEM((5, faces, rows, cells), f32),
-            pltpu.VMEM((5, faces, rows, cells), f32),
-            pltpu.VMEM((5, done + 1, rows, cells), f32),
+        return part_work(rows, faces, whole, done) + [
             pltpu.VMEM((5, done, rows, cells), f32),
             pltpu.SemaphoreType.DMA((5,)),
         ]
@@ -490,18 +455,18 @@
     *partial, border = pl.pallas_call(
         z_most_kernel,
         out_shape=results + (jax.ShapeDtypeStruct((5, rows, cells), f32),),
-        in_specs=[vmem, vmem],
+        in_specs=[hbm, vmem, vmem],
         out_specs=(hbm, hbm, hbm, vmem),
         scratch_shapes=z_work(most + 1, planes + WIDTH, most),
         compiler_params=params,
         name="z_sweep_most",
-    )(main, first)
+    )(boundary, main, first)
     return pl.pallas_call(
         z_rest_kernel,
         out_shape=results,
         in_specs=[hbm, vmem, vmem, vmem, hbm, hbm, hbm],
         out_specs=(hbm, hbm, hbm),
-        scratch_shapes=[flags] + z_work(WIDTH, planes, WIDTH),
+        scratch_shapes=z_work(WIDTH, planes, WIDTH),
         input_output_aliases={4: 0, 5: 1, 6: 2},
         compiler_params=params,
         name="z_sweep_rest",

time: 37.3 us -> 36.8 us (0.987)
  waiting for transfers between devices: 20.3 us -> 19.6 us
    ppermute x4, waiting for transfers between devices: 20.3 us -> 19.6 us  [swap(): return lax.ppermute(block, ('gz', 'row'), pairs)]
    pallas_call x1 -> x2, Pallas kernels: 0.92 us -> 1.09 us  [the longest x1 0.64 us: on_device(): pl.pallas_call(y_most_kernel, out_shape=(jax.ShapeDtypeStruct((5, most, p...]
  transfers between devices with their start and end apart: 4 -> 4, of which waited for: 3 -> 3; matrix products, arithmetic and copies ran while one was open for 0% -> 0% of each run, Pallas kernels for 4% -> 5%
where the time goes in v4:
time: 36.8 us; the launch traced here: 36.6 us
  waiting for transfers between devices  19.6 us (53%)
  starting transfers between devices  10.4 us (28%)
  Pallas kernels  5.91 us (16%)
  between operations  0.71 us (2%)
    ppermute x4, waiting for transfers between devices, swap(): return lax.ppermute(block, ('gz', 'row'), pairs)  19.6 us
    ppermute x4, starting transfers between devices, swap(): return lax.ppermute(block, ('gz', 'row'), pairs)  10.4 us
    pallas_call x1, Pallas kernels, on_device(): pl.pallas_call(x_kernel, out_shape=(by_y, y_edge, y_edge), in_specs=[hbm,...  2.44 us
    pallas_call x1, Pallas kernels, on_device(): pl.pallas_call(z_most_kernel, out_shape=results + (jax.ShapeDtypeStruct((...  1.34 us
    pallas_call x1, Pallas kernels, on_device(): pl.pallas_call(z_rest_kernel, out_shape=results, in_specs=[hbm, vmem, vme...  1.04 us
  transfers between devices with their start and end apart: 4, of which 3 were waited for; matrix products, arithmetic and copies ran while one was open for 0% of the time, Pallas kernels for 5%

profile of v4, /device:TPU:376, one launch (start us, length us, event | category | flops | bytes accessed | tf_op | source)
XLA Modules:
  0.0 36.6 jit_solution(1894914329015534827)
XLA Ops:
  0.6 2.4 %x_sweep.1 = (f32[5,8,8,256]{3,2,1,0:T(8,128)S(1)}, f32[5,3,8,256]{3,2,1,0:T(8,128)S(1)}, f32[5,3,8,256]{3,2,1,0:T(8,128)S(1)}) custom-call(s32[6]{0:T(128)} %bounds.9, f32[8,8,256]{2,1,0:T(8,128)} %dens.1, f32[8,8,256]{2,1,0:T(8,128)} %press.1, f32[3,8,8,256]{3,2,1,0:T(8,128)} %vel.1), custom_call_target="tpu_custom_call" | custom-call | tf_op jit(solution)/shard_map/x_sweep/pallas_call | solution.py:398
  3.1 1.9 %collective-permute-start.1 = (f32[5,3,8,256]{3,2,1,0:T(8,128)S(1)}, f32[5,3,8,256]{3,2,1,0:T(8,128)S(1)}, u32[]{:S(2)}, u32[]{:S(2)}) collective-permute-start(f32[5,3,8,256]{3,2,1,0:T(8,128)S(1)} %get-tuple-element.17), channel_id=1, source_target_pairs={{1,2},{2,1},{3,4},{4,3},{5,6},{6,5},{7,8},{8,7},{9,10},{10,9},{11,... | collective-permute-start | bytes 368648 | tf_op jit(solution)/shard_map/ppermute | solution.py:355
  5.0 0.0 copy-start
  5.0 3.8 %collective-permute-start = (f32[5,3,8,256]{3,2,1,0:T(8,128)S(1)}, f32[5,3,8,256]{3,2,1,0:T(8,128)S(1)}, u32[]{:S(2)}, u32[]{:S(2)}) collective-permute-start(f32[5,3,8,256]{3,2,1,0:T(8,128)S(1)} %get-tuple-element.16), channel_id=1, source_target_pairs={{0,1},{1,0},{2,3},{3,2},{4,5},{5,4},{6,7},{7,6},{8,9},{9,8},{10,11... | collective-permute-start | bytes 368648 | tf_op jit(solution)/shard_map/ppermute | solution.py:355
  8.9 0.0 collective-permute-done.1.first
  8.9 0.0 copy-done
  8.9 0.6 %y_sweep_most.1 = (f32[5,5,8,256]{3,2,1,0:T(8,128)S(1)}, f32[5,8,256]{2,1,0:T(8,128)S(1)}) custom-call(s32[6]{0:T(128)S(1)} %copy-done, f32[5,8,8,256]{3,2,1,0:T(8,128)S(1)} %get-tuple-element.15.main, f32[5,3,8,256]{3,2,1,0:T(8,128)S(1)} %collective-permute-done.1.first), custom_call_target="tpu_custom_call" | custom-call | tf_op jit(solution)/shard_map/y_sweep_most/pallas_call | solution.py:418
  9.5 12.8 %collective-permute-done.second = f32[5,3,8,256]{3,2,1,0:T(8,128)S(1)} collective-permute-done((f32[5,3,8,256]{3,2,1,0:T(8,128)S(1)}, f32[5,3,8,256]{3,2,1,0:T(8,128)S(1)}, u32[]{:S(2)}, u32[]{:S(2)}) %collective-permute-start) | collective-permute-done | bytes 122912 | tf_op jit(solution)/shard_map/ppermute | solution.py:355
  22.3 0.4 %y_sweep_rest.1 = (f32[5,8,8,256]{3,2,1,0:T(8,128)S(1)}, f32[5,3,8,256]{3,2,1,0:T(8,128)S(1)}, f32[5,3,8,256]{3,2,1,0:T(8,128)S(1)}) custom-call(s32[6]{0:T(128)S(1)} %copy-done, f32[5,8,8,256]{3,2,1,0:T(8,128)S(1)} %get-tuple-element.15.main, f32[5,3,8,256]{3,2,1,0:T(8,128)S(1)} %collective-permute-done.second, f32[5,8,256]{2,1,0:T(8,128)S(1)} %get-tuple-element.18.border, ...), custom_call_target="tpu_custom_call" | custom-call | tf_op jit(solution)/shard_map/y_sweep_rest/pallas_call | solution.py:430
  22.8 2.7 %collective-permute-start.3 = (f32[5,3,8,256]{3,2,1,0:T(8,128)S(1)}, f32[5,3,8,256]{3,2,1,0:T(8,128)S(1)}, u32[]{:S(2)}, u32[]{:S(2)}) collective-permute-start(f32[5,3,8,256]{3,2,1,0:T(8,128)S(1)} %get-tuple-element.22), channel_id=1, source_target_pairs={{0,16},{16,0},{1,17},{17,1},{2,18},{18,2},{3,19},{19,3},{4,20},{20... | collective-permute-start | bytes 368648 | tf_op jit(solution)/shard_map/ppermute | solution.py:355
  25.4 2.0 %collective-permute-start.2 = (f32[5,3,8,256]{3,2,1,0:T(8,128)S(1)}, f32[5,3,8,256]{3,2,1,0:T(8,128)S(1)}, u32[]{:S(2)}, u32[]{:S(2)}) collective-permute-start(f32[5,3,8,256]{3,2,1,0:T(8,128)S(1)} %get-tuple-element.21), channel_id=1, source_target_pairs={{16,32},{32,16},{17,33},{33,17},{18,34},{34,18},{19,35},{35,19},{2... | collective-permute-start | bytes 368648 | tf_op jit(solution)/shard_map/ppermute | solution.py:355
  27.4 2.1 %collective-permute-done.3.first = f32[5,3,8,256]{3,2,1,0:T(8,128)S(1)} collective-permute-done((f32[5,3,8,256]{3,2,1,0:T(8,128)S(1)}, f32[5,3,8,256]{3,2,1,0:T(8,128)S(1)}, u32[]{:S(2)}, u32[]{:S(2)}) %collective-permute-start.3) | collective-permute-done | bytes 122912 | tf_op jit(solution)/shard_map/ppermute | solution.py:355
  29.6 1.3 %z_sweep_most.1 = (f32[8,8,256]{2,1,0:T(8,128)}, f32[8,8,256]{2,1,0:T(8,128)}, f32[3,8,8,256]{3,2,1,0:T(8,128)}, f32[5,8,256]{2,1,0:T(8,128)S(1)}) custom-call(s32[6]{0:T(128)S(1)} %copy-done, f32[5,8,8,256]{3,2,1,0:T(8,128)S(1)} %get-tuple-element.20.main, f32[5,3,8,256]{3,2,1,0:T(8,128)S(1)} %collective-permute-done.3.first), custom_call_target="tpu_custom_call" | custom-call | tf_op jit(solution)/shard_map/z_sweep_most/pallas_call | solution.py:455
  30.9 4.6 %collective-permute-done.2.second = f32[5,3,8,256]{3,2,1,0:T(8,128)S(1)} collective-permute-done((f32[5,3,8,256]{3,2,1,0:T(8,128)S(1)}, f32[5,3,8,256]{3,2,1,0:T(8,128)S(1)}, u32[]{:S(2)}, u32[]{:S(2)}) %collective-permute-start.2) | collective-permute-done | bytes 122912 | tf_op jit(solution)/shard_map/ppermute | solution.py:355
  35.5 1.0 %z_sweep_rest.1 = (f32[8,8,256]{2,1,0:T(8,128)}, f32[8,8,256]{2,1,0:T(8,128)}, f32[3,8,8,256]{3,2,1,0:T(8,128)}) custom-call(s32[6]{0:T(128)S(1)} %copy-done, f32[5,8,8,256]{3,2,1,0:T(8,128)S(1)} %get-tuple-element.20.main, f32[5,3,8,256]{3,2,1,0:T(8,128)S(1)} %collective-permute-done.2.second, ...), custom_call_target="tpu_custom_call", output_to_operand_aliasing={{0}: (4, {}), {1}: (5, {}), {2}: (6, {})} | custom-call | tf_op jit(solution)/shard_map/z_sweep_rest/pallas_call | solution.py:464
Async XLA Ops:
  3.1 5.8 %collective-permute-start.1 = (f32[5,3,8,256]{3,2,1,0:T(8,128)S(1)}, f32[5,3,8,256]{3,2,1,0:T(8,128)S(1)}, u32[]{:S(2)}, u32[]{:S(2)}) collective-permute-start(f32[5,3,8,256]{3,2,1,0:T(8,128)S(1)} %get-tuple-element.17), channel_id=1, source_target_pairs={{1,2},{2,1},{3,4},{4,3},{5,6},{6,5},{7,8},{8,7},{9,10},{10,9},{11,... | collective-permute-start | bytes 368648 | tf_op jit(solution)/shard_map/ppermute | solution.py:355
  5.0 3.9 %copy-start = (s32[6]{0:T(128)S(1)}, s32[6]{0:T(128)}, u32[]{:S(2)}) copy-start(s32[6]{0:T(128)} %bounds.9) | copy-start | bytes 76
  5.0 17.3 %collective-permute-start = (f32[5,3,8,256]{3,2,1,0:T(8,128)S(1)}, f32[5,3,8,256]{3,2,1,0:T(8,128)S(1)}, u32[]{:S(2)}, u32[]{:S(2)}) collective-permute-start(f32[5,3,8,256]{3,2,1,0:T(8,128)S(1)} %get-tuple-element.16), channel_id=1, source_target_pairs={{0,1},{1,0},{2,3},{3,2},{4,5},{5,4},{6,7},{7,6},{8,9},{9,8},{10,11... | collective-permute-start | bytes 368648 | tf_op jit(solution)/shard_map/ppermute | solution.py:355
  22.8 6.8 %collective-permute-start.3 = (f32[5,3,8,256]{3,2,1,0:T(8,128)S(1)}, f32[5,3,8,256]{3,2,1,0:T(8,128)S(1)}, u32[]{:S(2)}, u32[]{:S(2)}) collective-permute-start(f32[5,3,8,256]{3,2,1,0:T(8,128)S(1)} %get-tuple-element.22), channel_id=1, source_target_pairs={{0,16},{16,0},{1,17},{17,1},{2,18},{18,2},{3,19},{19,3},{4,20},{20... | collective-permute-start | bytes 368648 | tf_op jit(solution)/shard_map/ppermute | solution.py:355
  25.4 10.1 %collective-permute-start.2 = (f32[5,3,8,256]{3,2,1,0:T(8,128)S(1)}, f32[5,3,8,256]{3,2,1,0:T(8,128)S(1)}, u32[]{:S(2)}, u32[]{:S(2)}) collective-permute-start(f32[5,3,8,256]{3,2,1,0:T(8,128)S(1)} %get-tuple-element.21), channel_id=1, source_target_pairs={{16,32},{32,16},{17,33},{33,17},{18,34},{34,18},{19,35},{35,19},{2... | collective-permute-start | bytes 368648 | tf_op jit(solution)/shard_map/ppermute | solution.py:355
